TPU v7x, 512 devices: a whole 4x8x8 slice. The times are simulated.
512 devices in a mesh: doc: 16 (over y_hi, z), ctx: 32 (over x, y_lo, core).
Axes of the slice: x: 4, y: 8 (y_hi: 2, y_lo: 4; y = y_hi * 4 + y_lo), z: 8, core: 2. Of those that a mesh axis runs over, the one named last changes fastest.
Arguments:
- queries: bfloat16 [16, 4096, 4096], P('doc', 'ctx'), may hold values from -6 to 6
- out_grad: bfloat16 [16, 4096, 4096], P('doc', 'ctx'), may hold values from -6 to 6
- mem_keys: bfloat16 [16, 64, 4096], P('doc', 'ctx'), may hold values from -6 to 6
- mem_values: bfloat16 [16, 64, 4096], P('doc', 'ctx'), may hold values from -6 to 6
Outputs:
- grad_queries: float32 [16, 4096, 4096], P('doc', 'ctx')
- grad_keys: float32 [16, 64, 4096], P('doc', 'ctx')
- grad_values: float32 [16, 64, 4096], P('doc', 'ctx')
All inputs are finite; a program needn't handle non-finite values.
Results may differ from a plain program's by a relative error of at most 0.0011.
Values may be sent and summed in bfloat16 or wider, within the bound.
No kernel may reach another device: no remote copies, remote signals or barrier semaphores. Data moves between devices by JAX's collectives and lax.ppermute only.
A program may use at most 64 MiB of HBM per device.

v0:
```python
import jax
import jax.numpy as jnp
from jax import lax
from jax.sharding import PartitionSpec as P

HD = 128


def heads_view(block):
    return block.reshape(block.shape[0], block.shape[1] // HD, HD)


def score_pair(q_block, g_block, k_rows, v_rows):
    scores = jnp.einsum("qhd,khd->hqk", q_block, k_rows, preferred_element_type=jnp.float32)
    expo = jnp.exp(scores * HD ** (-0.5))
    dprob = jnp.einsum("qhd,khd->hqk", g_block, v_rows, preferred_element_type=jnp.float32)
    return (expo, dprob)


def grads_from(q_block, g_block, k_rows, expo, dprob, norm, drift):
    high = lax.Precision.HIGHEST
    scale = HD ** (-0.5)
    prob = expo / norm[:, :, None]
    dscore = prob * (dprob - drift[:, :, None])
    grad_q = jnp.einsum("hqk,khd->qhd", dscore, k_rows.astype(jnp.float32), precision=high) * scale
    grad_k = jnp.einsum("hqk,qhd->khd", dscore, q_block.astype(jnp.float32), precision=high) * scale
    grad_v = jnp.einsum("hqk,qhd->khd", prob, g_block.astype(jnp.float32), precision=high)
    return (grad_q, grad_k, grad_v)


def shards(queries, out_grad, mem_keys, mem_values):
    q_heads, g_heads, k_heads, v_heads = (
        lax.all_to_all(queries, "ctx", split_axis=2, concat_axis=1, tiled=True),
        lax.all_to_all(out_grad, "ctx", split_axis=2, concat_axis=1, tiled=True),
        lax.all_to_all(mem_keys, "ctx", split_axis=2, concat_axis=1, tiled=True),
        lax.all_to_all(mem_values, "ctx", split_axis=2, concat_axis=1, tiled=True),
    )
    q_rows = heads_view(q_heads[0])
    g_rows = heads_view(g_heads[0])
    qlen, nheads = (q_rows.shape[0], q_rows.shape[1])
    mem_rows = k_heads.shape[1]
    width = nheads * HD
    ndoc = lax.axis_size("doc")
    total = ndoc * mem_rows
    block = min(qlen, 512)
    nblock = qlen // block
    q_blocks = q_rows.reshape(nblock, block, nheads, HD)
    g_blocks = g_rows.reshape(nblock, block, nheads, HD)
    k_all, v_all = (
        lax.all_gather(k_heads[0], "doc", axis=0, tiled=True),
        lax.all_gather(v_heads[0], "doc", axis=0, tiled=True),
    )
    k_rows = heads_view(k_all)
    v_rows = heads_view(v_all)

    def whole_block(accum, items):
        expo, dprob = score_pair(items[0], items[1], k_rows, v_rows)
        norm = jnp.sum(expo, axis=2)
        drift = jnp.sum(expo * dprob, axis=2) / norm
        grad_q, grad_k, grad_v = grads_from(items[0], items[1], k_rows, expo, dprob, norm, drift)
        return ((accum[0] + grad_k, accum[1] + grad_v), grad_q)

    zero_all = jnp.zeros((total, nheads, HD), jnp.float32)
    sums, grad_q = lax.scan(whole_block, (zero_all, zero_all), (q_blocks, g_blocks))
    grad_k, grad_v = (
        lax.psum_scatter(sums[0].reshape(total, width), "doc", scatter_dimension=0, tiled=True),
        lax.psum_scatter(sums[1].reshape(total, width), "doc", scatter_dimension=0, tiled=True),
    )
    grad_q = grad_q.reshape(qlen, width)
    return (
        lax.all_to_all(grad_q[None], "ctx", split_axis=1, concat_axis=2, tiled=True),
        lax.all_to_all(grad_k[None], "ctx", split_axis=1, concat_axis=2, tiled=True),
        lax.all_to_all(grad_v[None], "ctx", split_axis=1, concat_axis=2, tiled=True),
    )


def solution(mesh):
    placed = (
        P("doc", "ctx", None),
        P("doc", "ctx", None),
        P("doc", "ctx", None),
        P("doc", "ctx", None),
    )
    return jax.shard_map(
        shards,
        mesh=mesh,
        in_specs=placed,
        out_specs=(P("doc", "ctx", None), P("doc", "ctx", None), P("doc", "ctx", None)),
        check_vma=False,
    )
```

profile of v0, /device:TPU:1, one launch (start us, length us, event | category | flops | bytes accessed | tf_op | source)
XLA Modules:
  0.0 856.9 jit_solution(1877382653145196616)
XLA Ops:
  7.2 4.3 copy.61
  12.0 22.5 %reduce.5 = bf16[4096,2]{1,0:T(8,128)(2,1)S(1)} reduce(bf16[4096,1,2]{2,1,0:T(2,128)(2,1)S(1)} %bitcast.136, bf16[]{:T(256)} %broadcast.43), dimensions={1}, to_apply=%bitcast.91.reduce_sub_computation | reduce | bytes 32770
  34.5 2.2 reshape.90
  36.7 10.3 %all-to-all-start.1 = ((bf16[32,2,128]{2,1,0:T(2,128)(2,1)}), bf16[32,2,128]{2,1,0:T(2,128)(2,1)S(1)}, u32[]{:S(2)}, u32[]{:S(2)}) async-start(bf16[32,2,128]{2,1,0:T(2,128)(2,1)} %reshape.90), calls=%async_computation.1 | async-start | bytes 32768 | tf_op jit(solution)/shard_map/all_to_all | solution.py:35
  47.0 2.7 copy.66
  49.7 22.5 %reduce.7 = bf16[4096,2]{1,0:T(8,128)(2,1)S(1)} reduce(bf16[4096,1,2]{2,1,0:T(2,128)(2,1)S(1)} %bitcast.141, bf16[]{:T(256)} %broadcast.43), dimensions={1}, to_apply=%bitcast.95.reduce_sub_computation | reduce | bytes 32770
  72.2 2.2 reshape.94
  74.4 7.8 all-to-all-start.3
  82.2 5.0 copy.59
  87.3 22.4 %reduce.4 = bf16[4096,128]{1,0:T(8,128)(2,1)S(1)} reduce(bf16[4096,1,128]{2,1,0:T(2,128)(2,1)S(1)} %bitcast.142, bf16[]{:T(256)} %broadcast.43), dimensions={1}, to_apply=%bitcast.89.reduce_sub_computation | reduce | bytes 2097154
  110.8 7.7 all-to-all-start
  118.5 5.0 copy.64
  123.5 23.5 %reduce.6 = bf16[4096,128]{1,0:T(8,128)(2,1)} reduce(bf16[4096,1,128]{2,1,0:T(2,128)(2,1)S(1)} %bitcast.137, bf16[]{:T(256)} %broadcast.43), dimensions={1}, to_apply=%bitcast.93.reduce_sub_computation | reduce | bytes 2097154
  147.0 2.2 reshape.92
  149.2 7.7 all-to-all-start.2
  157.3 2.5 reshape.91
  159.7 2.0 copy.62
  161.7 2.5 reshape.95
  164.2 2.0 copy.67
  166.2 49.7 %all_gather.6 = bf16[1024,128]{1,0:T(8,128)(2,1)S(1)} all-gather(bf16[64,128]{1,0:T(8,128)(2,1)S(1)} %bitcast.154), channel_id=1, replica_groups=mesh['doc'=16,'ctx'=32] {'doc'}, dimensions={0}, use_global_device_ids=true | all-gather | bytes 278528 | tf_op jit(solution)/shard_map/all_gather | solution.py:50
  215.9 41.2 %all_gather.7 = bf16[1024,128]{1,0:T(8,128)(2,1)S(1)} all-gather(bf16[64,128]{1,0:T(8,128)(2,1)S(1)} %bitcast.155), channel_id=1, replica_groups=mesh['doc'=16,'ctx'=32] {'doc'}, dimensions={0}, use_global_device_ids=true | all-gather | bytes 278528 | tf_op jit(solution)/shard_map/all_gather | solution.py:51
  257.1 4.3 reshape.89
  262.5 2.3 copy.60
  264.8 4.3 reshape.93
  270.2 1.7 copy.65
  271.9 58.5 %while.15 = (s32[]{:T(128)}, f32[1024,1,128]{0,2,1:T(8,128)S(1)}, f32[1024,1,128]{0,2,1:T(8,128)S(1)}, f32[8,512,1,128]{3,1,2,0:T(8,128)}, bf16[8,512,1,128]{3,1...) while((s32[]{:T(128)}, f32[1024,1,128]{0,2,1:T(8,128)S(1)}, ...), condition=%wide.region_3.4_spmd.clone, body=%wide.region_0.3_spmd.clone.sunk | while | flops 2689269248 | bytes 22560908 | solution.py:64
  272.3 1.6 fusion.44
  274.4 1.2 fusion.46
  275.5 1.9 fusion.45
  277.4 1.8 fusion.47
  279.6 1.6 fusion.44
  281.7 1.2 fusion.46
  282.8 1.9 fusion.45
  284.7 1.8 fusion.47
  287.0 1.6 fusion.44
  289.0 1.2 fusion.46
  290.1 1.9 fusion.45
  292.0 1.8 fusion.47
  294.3 1.6 fusion.44
  296.3 1.2 fusion.46
  297.4 1.9 fusion.45
  299.3 1.8 fusion.47
  301.6 1.6 fusion.44
  303.6 1.2 fusion.46
  304.7 1.9 fusion.45
  306.7 1.8 fusion.47
  308.9 1.6 fusion.44
  312.0 1.9 fusion.45
  314.0 1.8 fusion.47
  316.2 1.6 fusion.44
  318.2 1.2 fusion.46
  319.3 1.9 fusion.45
  321.3 1.8 fusion.47
  323.5 1.6 fusion.44
  326.7 1.9 fusion.45
  328.6 1.8 fusion.47
  332.5 222.8 %reduce-scatter.3.cloned.1.call-done = f32[64,128]{1,0:T(8,128)} async-done(((f32[1024,128]{1,0:T(8,128)}), f32[64,128]{1,0:T(8,128)}) %reduce-scatter.3.cloned.1.call-update) | async-done | bytes 32784 | tf_op jit(solution)/shard_map/reduce_scatter | solution.py:66
  555.3 10.4 %all-to-all-start.5 = ((f32[1,64,128]{2,0,1:T(1,128)}), f32[1,64,128]{2,0,1:T(1,128)S(1)}, u32[]{:S(2)}, u32[]{:S(2)}) async-start(f32[1,64,128]{2,0,1:T(1,128)} %bitcast.158), calls=%async_computation.6 | async-start | bytes 65536 | tf_op jit(solution)/shard_map/all_to_all | solution.py:72
  565.7 206.2 %reduce-scatter.5.cloned.1.call-done = f32[64,128]{1,0:T(8,128)} async-done(((f32[1024,128]{1,0:T(8,128)}), f32[64,128]{1,0:T(8,128)}) %reduce-scatter.5.cloned.1.call-update) | async-done | bytes 32784 | tf_op jit(solution)/shard_map/reduce_scatter | solution.py:67
  771.9 18.0 %all_to_all.114 = f32[1,64,128]{2,0,1:T(1,128)S(1)} all-to-all(f32[1,64,128]{2,0,1:T(1,128)} %bitcast.159), channel_id=1, replica_groups=mesh['doc'=16,'ctx'=32] {'ctx'}, dimensions={1} | all-to-all | bytes 65536 | tf_op jit(solution)/shard_map/all_to_all | solution.py:73
  789.9 4.2 all-to-all-start.4
  794.1 50.0 %all-to-all-done.4 = f32[1,4096,128]{2,0,1:T(1,128)S(1)} async-done(((f32[1,4096,128]{2,0,1:T(1,128)}), f32[1,4096,128]{2,0,1:T(1,128)S(1)}, u32[]{:S(2)}, u32[]{:S(2)}) %all-to-all-start.4) | async-done | bytes 2097184 | tf_op jit(solution)/shard_map/all_to_all | solution.py:71
  844.1 1.9 copy.71
  846.0 2.9 copy.74
  (56 shorter events, 16.4 us)
Async XLA Ops:
  12.0 35.0 %copy-start.2 = (bf16[1,2,4096]{2,1,0:T(2,128)(2,1)S(1)}, bf16[1,2,4096]{2,1,0:T(2,128)(2,1)}, u32[]{:S(2)}) copy-start(bf16[1,2,4096]{2,1,0:T(2,128)(2,1)} %param.9) | copy-start | bytes 49156
  36.7 37.7 %all-to-all-start.1 = ((bf16[32,2,128]{2,1,0:T(2,128)(2,1)}), bf16[32,2,128]{2,1,0:T(2,128)(2,1)S(1)}, u32[]{:S(2)}, u32[]{:S(2)}) async-start(bf16[32,2,128]{2,1,0:T(2,128)(2,1)} %reshape.90), calls=%async_computation.1 | async-start | bytes 32768 | tf_op jit(solution)/shard_map/all_to_all | solution.py:35
  74.4 36.4 %all-to-all-start.3 = ((bf16[32,2,128]{2,1,0:T(2,128)(2,1)}), bf16[32,2,128]{2,1,0:T(2,128)(2,1)S(1)}, u32[]{:S(2)}, u32[]{:S(2)}) async-start(bf16[32,2,128]{2,1,0:T(2,128)(2,1)} %reshape.94), calls=%async_computation.3 | async-start | bytes 32768 | tf_op jit(solution)/shard_map/all_to_all | solution.py:36
  110.8 38.4 %all-to-all-start = ((bf16[32,2,8192]{2,1,0:T(2,128)(2,1)}), bf16[32,2,8192]{2,1,0:T(2,128)(2,1)S(1)}, u32[]{:S(2)}, u32[]{:S(2)}) async-start(bf16[32,2,8192]{2,1,0:T(2,128)(2,1)} %reshape.88), calls=%async_computation | async-start | bytes 2097152 | tf_op jit(solution)/shard_map/all_to_all | solution.py:33
  149.2 8.1 copy-start
  149.2 115.6 %all-to-all-start.2 = ((bf16[32,2,8192]{2,1,0:T(2,128)(2,1)}), bf16[32,2,8192]{2,1,0:T(2,128)(2,1)}, u32[]{:S(2)}, u32[]{:S(2)}) async-start(bf16[32,2,8192]{2,1,0:T(2,128)(2,1)} %reshape.92), calls=%async_computation.2 | async-start | bytes 2097152 | tf_op jit(solution)/shard_map/all_to_all | solution.py:34
  156.9 398.4 %reduce-scatter.3.cloned.1.call-start = ((), (), s32[]{:S(2)}) async-start(), calls=%async_computation.9 | async-start | bytes 557056 | tf_op jit(solution)/shard_map/reduce_scatter | solution.py:66
  270.2 1.7 copy-start.1
  331.4 440.6 %reduce-scatter.5.cloned.1.call-start = ((), (), s32[]{:S(2)}) async-start(), calls=%async_computation.10 | async-start | bytes 557056 | tf_op jit(solution)/shard_map/reduce_scatter | solution.py:67
  555.3 216.7 %all-to-all-start.5 = ((f32[1,64,128]{2,0,1:T(1,128)}), f32[1,64,128]{2,0,1:T(1,128)S(1)}, u32[]{:S(2)}, u32[]{:S(2)}) async-start(f32[1,64,128]{2,0,1:T(1,128)} %bitcast.158), calls=%async_computation.6 | async-start | bytes 65536 | tf_op jit(solution)/shard_map/all_to_all | solution.py:72
  789.9 54.2 %all-to-all-start.4 = ((f32[1,4096,128]{2,0,1:T(1,128)}), f32[1,4096,128]{2,0,1:T(1,128)S(1)}, u32[]{:S(2)}, u32[]{:S(2)}) async-start(f32[1,4096,128]{2,0,1:T(1,128)} %bitcast.147), calls=%async_computation.4 | async-start | bytes 4194304 | tf_op jit(solution)/shard_map/all_to_all | solution.py:71
Sparse Core Ops, SparseCore 0:
  331.5 223.7 reduce-scatter.2
  559.7 212.2 reduce-scatter.4
where the time goes:
time: 858 us; the launch traced here: 857 us
  waiting for transfers between devices  479 us (56%)
  blocking collectives  109 us (13%)
  other arithmetic  93.9 us (11%)
  local copies, waits for them, and re-layouts  56.9 us (7%)
  matrix products  55.2 us (6%)
  starting transfers between devices  48.5 us (6%)
  between operations  14.3 us (2%)
    reduce_scatter x1, waiting for transfers between devices, shards(): lax.psum_scatter(sums[0].reshape(total, width), 'doc', scatter_dimension=...  223 us
    reduce_scatter x1, waiting for transfers between devices, shards(): lax.psum_scatter(sums[1].reshape(total, width), 'doc', scatter_dimension=...  206 us
    unnamed x6, other arithmetic  90.8 us
    all_to_all x1, waiting for transfers between devices, shards(): lax.all_to_all(grad_q[None], 'ctx', split_axis=1, concat_axis=2, tiled=True)  50 us
    all_gather x1, blocking collectives, shards(): lax.all_gather(k_heads[0], 'doc', axis=0, tiled=True)  49.7 us
    unnamed x26, local copies, waits for them, and re-layouts  45.1 us
    all_gather x1, blocking collectives, shards(): lax.all_gather(v_heads[0], 'doc', axis=0, tiled=True)  41.2 us
    all_to_all x1, blocking collectives, shards(): lax.all_to_all(grad_v[None], 'ctx', split_axis=1, concat_axis=2, tiled=True)  18 us
  transfers between devices with their start and end apart: 8, of which 3 were waited for; matrix products, arithmetic and copies ran while one was open for 12% of the time, Pallas kernels for 0%

commit v1 on v0

v1 whole, which is shorter than its diff:
```python
import jax
import jax.numpy as jnp
from jax import lax
from jax.experimental import pallas as pl
from jax.experimental.pallas import tpu as pltpu
from jax.sharding import PartitionSpec as P


HD = 128
SCALE = HD ** (-0.5)
CHUNKS = (96, 32)
QBLOCK = 512
TILE = 8
HALF_BITS = 14.0
F32 = jnp.float32
BF16 = jnp.bfloat16
HALF = jnp.float16


def dot(a, b, da, db):
    return lax.dot_general(a, b, (((da,), (db,)), ((), ())), preferred_element_type=F32)


def split(x):
    hi = x.astype(BF16)
    return hi, (x - hi.astype(F32)).astype(BF16)


def exponent(top):
    return jnp.ceil(jnp.log2(jnp.maximum(top, 1e-30))) - HALF_BITS


def by_head(queries, out_grad, mem_keys, mem_values, chunks):
    rows, width = queries.shape
    mem = mem_keys.shape[0]
    nheads = width // HD
    group = min(nheads, 8)

    def kernel(q_ref, g_ref, k_ref, v_ref, *outs):
        k = k_ref[...].astype(F32)
        v = v_ref[...].astype(F32)
        fill = jnp.zeros((TILE - 2 * mem, HD), F32)
        for h in range(group):
            cols = slice(h * HD, (h + 1) * HD)
            start = 0
            for out, part in zip(outs, chunks):
                out[h, :part, :] = q_ref[start:start + part, cols]
                out[h, part:2 * part, :] = g_ref[start:start + part, cols]
                start += part
            outs[0][h, 2 * chunks[0]:, :] = jnp.concatenate([k[:, cols], v[:, cols], fill], axis=0).astype(BF16)

    sizes = [2 * part + (TILE if c == 0 else 0) for c, part in enumerate(chunks)]
    return pl.pallas_call(
        kernel,
        grid=(nheads // group,),
        in_specs=[pl.BlockSpec((rows, group * HD), lambda i: (0, i))] * 2
        + [pl.BlockSpec((mem, group * HD), lambda i: (0, i))] * 2,
        out_specs=[pl.BlockSpec((group, size, HD), lambda i: (i, 0, 0)) for size in sizes],
        out_shape=[jax.ShapeDtypeStruct((nheads, size, HD), BF16) for size in sizes],
        cost_estimate=pl.CostEstimate(flops=0, bytes_accessed=8 * rows * width, transcendentals=0),
        name="by_head",
    )(queries, out_grad, mem_keys, mem_values)


def memory_copies(block, part, rows, ndoc):
    ndev = block.shape[0]
    total = ndev * rows

    def kernel(x_ref, out, tmp):
        x = x_ref[...].astype(F32)
        for c in range(ndev):
            tmp[c * rows:(c + 1) * rows, :] = x[c, :rows, :]
            tmp[total + c * rows:total + (c + 1) * rows, :] = x[c, rows:2 * rows, :]
        whole = tmp[...].astype(BF16)
        for d in range(ndoc):
            out[d] = whole

    return pl.pallas_call(
        kernel,
        grid=(1,),
        in_specs=[pl.BlockSpec((ndev, TILE, HD), lambda i: (0, 2 * part // TILE, 0))],
        out_specs=pl.BlockSpec((ndoc, 2 * total, HD), lambda i: (0, 0, 0)),
        out_shape=jax.ShapeDtypeStruct((ndoc, 2 * total, HD), BF16),
        scratch_shapes=[pltpu.VMEM((2 * total, HD), F32)],
        cost_estimate=pl.CostEstimate(flops=0, bytes_accessed=4 * ndoc * total * HD, transcendentals=0),
        compiler_params=pltpu.CompilerParams(vmem_limit_bytes=4 << 20),
        name="memory_copies",
    )(block)


def attention_grads(rows, part, memory, before, last):
    ndev = rows.shape[0]
    ndoc, both_mem, _ = memory.shape
    mem = both_mem // 2
    total = ndoc * mem
    per = max(1, min(ndev, QBLOCK // part))
    while ndev % per:
        per -= 1
    block = per * part
    steps = ndev // per
    size = both_mem + (TILE if last else 0)

    def kernel(*refs):
        if before is None:
            x_ref, m_ref, gq_ref, power_ref, sums_ref, k_ref, v_ref, top_ref = refs
        else:
            x_ref, m_ref, before_ref, gq_ref, power_ref, sums_ref, k_ref, v_ref, top_ref = refs
        acc_ref = sums_ref.at[:, :both_mem, :]
        step = pl.program_id(0)

        @pl.when(step == 0)
        def _():
            acc_ref[...] = jnp.zeros_like(acc_ref) if before is None else before_ref[...]
            k_ref[...] = m_ref[:, :mem, :].reshape(total, HD)
            v_ref[...] = m_ref[:, mem:, :].reshape(total, HD)
            top_ref[...] = jnp.zeros_like(top_ref)

        q = x_ref[:, :part, :].reshape(block, HD)
        g = x_ref[:, part:2 * part, :].reshape(block, HD)
        k = k_ref[...]
        v = v_ref[...]
        expo = jnp.exp(dot(k, q, 1, 1) * SCALE)
        dprob = dot(v, g, 1, 1)
        norm = jnp.sum(expo, axis=0, keepdims=True)
        drift = jnp.sum(expo * dprob, axis=0, keepdims=True) / norm
        prob = expo * (1.0 / norm)
        dscore = prob * (dprob - drift)
        p_hi, p_lo = split(prob)
        s_hi, s_lo = split(dscore)
        grad_v = dot(p_hi, g, 1, 0) + dot(p_lo, g, 1, 0)
        grad_k = (dot(s_hi, q, 1, 0) + dot(s_lo, q, 1, 0)) * SCALE
        grad_q = (dot(s_hi, k, 0, 0) + dot(s_lo, k, 0, 0)) * SCALE
        gq_ref[pl.ds(pl.multiple_of(step * block, block), block), :] = grad_q
        top_ref[...] = jnp.maximum(top_ref[...], jnp.max(jnp.abs(grad_q), axis=0, keepdims=True))
        acc_ref[:, :mem, :] += grad_k.reshape(ndoc, mem, HD)
        acc_ref[:, mem:, :] += grad_v.reshape(ndoc, mem, HD)

        @pl.when(step == steps - 1)
        def _():
            power = exponent(jnp.max(top_ref[...], axis=1, keepdims=True))
            gq_ref[...] = gq_ref[...] * jnp.exp2(-power)
            power_ref[...] = jnp.broadcast_to(power, power_ref.shape)
            if last:
                first = lax.broadcasted_iota(jnp.int32, (TILE, HD), 0) == 0
                powers = []
                for start in (0, mem):
                    x = acc_ref[:, start:start + mem, :]
                    top = jnp.max(jnp.max(jnp.max(jnp.abs(x), axis=0), axis=0, keepdims=True), axis=1, keepdims=True)
                    power = exponent(top)
                    acc_ref[:, start:start + mem, :] = x * jnp.exp2(-power).reshape(1, 1, 1)
                    powers.append(jnp.broadcast_to(power, (TILE, HD)))
                tail = jnp.where(first, powers[0], powers[1])
                for d in range(ndoc):
                    sums_ref[d, both_mem:, :] = tail

    def whole(*shape):
        return pl.BlockSpec(shape, lambda i: (0,) * len(shape))

    args = (rows, memory) if before is None else (rows, memory, before)
    return pl.pallas_call(
        kernel,
        grid=(steps,),
        in_specs=[pl.BlockSpec((per, 2 * part, HD), lambda i: (i, 0, 0))]
        + [whole(ndoc, both_mem, HD)] * (len(args) - 1),
        out_specs=[whole(ndev * part, HD), whole(1, HD), whole(ndoc, size, HD)],
        out_shape=[
            jax.ShapeDtypeStruct((ndev * part, HD), F32),
            jax.ShapeDtypeStruct((1, HD), F32),
            jax.ShapeDtypeStruct((ndoc, size, HD), F32),
        ],
        scratch_shapes=[pltpu.VMEM((total, HD), BF16)] * 2 + [pltpu.VMEM((1, HD), F32)],
        cost_estimate=pl.CostEstimate(
            flops=16 * ndev * part * total * HD,
            bytes_accessed=8 * ndev * part * HD,
            transcendentals=ndev * part * total,
        ),
        compiler_params=pltpu.CompilerParams(vmem_limit_bytes=24 << 20),
        name="attention_grads",
    )(*args)


def memory_sums(parts, powers, ndev):
    ndoc = parts.shape[0]
    mem = (parts.shape[1] - TILE) // 2
    rows = mem // ndev

    def kernel(x_ref, *refs):
        out = refs[-1]
        terms = []
        last = [p[...] for p in refs[:-1]]
        for v in (0, 1):
            total = jnp.zeros((mem, HD), F32)
            for d in range(ndoc):
                total = total + x_ref[d, v * mem:(v + 1) * mem, :] * jnp.exp2(x_ref[d, 2 * mem + v:2 * mem + v + 1, :])
            top = jnp.max(jnp.max(jnp.abs(total), axis=0, keepdims=True), axis=1, keepdims=True)
            power = exponent(top)
            total = total * jnp.exp2(-power)
            high = total.astype(BF16).astype(F32)
            terms += [high, total - high]
            last.append(jnp.broadcast_to(power, (1, HD)))
        last = jnp.concatenate(last + [jnp.zeros((2 * TILE - 4 * rows - len(last), HD), F32)], axis=0)
        for c in range(ndev):
            for t, term in enumerate(terms):
                out[c, t * rows:(t + 1) * rows, :] = term[c * rows:(c + 1) * rows, :]
            out[c, 4 * rows:, :] = last

    return pl.pallas_call(
        kernel,
        out_shape=jax.ShapeDtypeStruct((ndev, 2 * TILE, HD), F32),
        cost_estimate=pl.CostEstimate(flops=0, bytes_accessed=4 * parts.size, transcendentals=0),
        compiler_params=pltpu.CompilerParams(vmem_limit_bytes=6 << 20),
        name="memory_sums",
    )(parts, *powers)


def memory_rows(tail, rows, at):
    nheads = tail.shape[0]

    def kernel(x_ref, k_ref, v_ref):
        for h in range(nheads):
            cols = slice(h * HD, (h + 1) * HD)
            scale = jnp.exp2(x_ref[h, at:at + 2, :])
            k_ref[:, cols] = (x_ref[h, :rows, :] + x_ref[h, rows:2 * rows, :]) * scale[:1]
            v_ref[:, cols] = (x_ref[h, 2 * rows:3 * rows, :] + x_ref[h, 3 * rows:4 * rows, :]) * scale[1:]

    return pl.pallas_call(
        kernel,
        out_shape=[jax.ShapeDtypeStruct((rows, nheads * HD), F32)] * 2,
        cost_estimate=pl.CostEstimate(flops=0, bytes_accessed=16 * nheads * TILE * HD, transcendentals=0),
        compiler_params=pltpu.CompilerParams(vmem_limit_bytes=4 << 20),
        name="memory_rows",
    )(tail)


def swap(x, axis):
    return lax.all_to_all(x, axis, split_axis=0, concat_axis=0, tiled=True)


def shards(queries, out_grad, mem_keys, mem_values):
    ndoc = lax.axis_size("doc")
    nctx = lax.axis_size("ctx")
    mem = mem_keys.shape[1]
    nchunks = len(CHUNKS)
    blocks = list(by_head(queries[0], out_grad[0], mem_keys[0], mem_values[0], CHUNKS))
    for i in range(nchunks):
        blocks[i] = swap(blocks[i], "ctx")
    memory = swap(memory_copies(blocks[0], CHUNKS[0], mem, ndoc), "doc")
    sums = None
    powers = []
    grads = []
    for i, (block, part) in enumerate(zip(blocks, CHUNKS)):
        grad_q, power, sums = attention_grads(block, part, memory, sums, i == nchunks - 1)
        powers.append(power)
        grads.append(grad_q.reshape(nctx, part, HD))
    sums = swap(sums.astype(HALF), "doc").astype(F32)
    grads[-1] = jnp.concatenate([grads[-1], memory_sums(sums, powers, nctx)], axis=1)
    for i in range(nchunks):
        grads[i] = swap(grads[i].astype(HALF), "ctx")
    tail = grads[-1][:, CHUNKS[-1]:, :].astype(F32)
    grad_k, grad_v = memory_rows(tail, mem, 4 * mem + nchunks)
    grad_q = []
    for i, part in enumerate(CHUNKS):
        scale = jnp.exp2(tail[:, 4 * mem + i, :])[:, None, :]
        grad_q.append(jnp.transpose(grads[i][:, :part, :].astype(F32) * scale, (1, 0, 2)).reshape(part, -1))
    return jnp.concatenate(grad_q, axis=0)[None], grad_k[None], grad_v[None]


def solution(mesh):
    placed = P("doc", "ctx", None)
    return jax.shard_map(
        shards,
        mesh=mesh,
        in_specs=(placed,) * 4,
        out_specs=(placed,) * 3,
        check_vma=False,
    )
```

time: 858 us -> 202 us (0.24)
  waiting for transfers between devices: 479 us -> 49.6 us
  other arithmetic: 93.9 us -> 4.57 us
  matrix products: 55.2 us -> 0 us
  local copies, waits for them, and re-layouts: 56.9 us -> 4.27 us
  Pallas kernels: 0 us -> 32.8 us
  blocking collectives: 109 us -> 79.5 us
  starting transfers between devices: 48.5 us -> 29.9 us
  between operations: 14.3 us -> 0.77 us
    reduce_scatter x2 -> x0, waiting for transfers between devices: 429 us -> none  [the longest x1 223 us: shards(): lax.psum_scatter(sums[0].reshape(total, width), 'doc', scatter_dimension=...]
    unnamed x6 -> x0, other arithmetic: 90.8 us -> none
    all_gather x2 -> x0, blocking collectives: 90.8 us -> none  [the longest x1 49.7 us: shards(): lax.all_gather(k_heads[0], 'doc', axis=0, tiled=True)]
    all_to_all x1 -> x2, blocking collectives: 18 us -> 79.5 us  [swap(): return lax.all_to_all(x, axis, split_axis=0, concat_axis=0, tiled=True)]
    dot_general x40 -> x0, matrix products: 55.2 us -> none  [the longest x8 15.3 us: grads_from(): jnp.einsum('hqk,qhd->khd', dscore, q_block.astype(jnp.float32), precision...]
    unnamed x26 -> x8, local copies, waits for them, and re-layouts: 45.1 us -> 4.27 us
    pallas_call x0 -> x6, Pallas kernels: none -> 32.8 us  [the longest x2 28 us: attention_grads(): pl.pallas_call(kernel, grid=(steps,), in_specs=[pl.BlockSpec((per, 2 * pa...]
    all_to_all x6 -> x4, starting transfers between devices: 48.2 us -> 29.9 us  [swap(): return lax.all_to_all(x, axis, split_axis=0, concat_axis=0, tiled=True)]
  transfers between devices with their start and end apart: 8 -> 4, of which waited for: 3 -> 3; matrix products, arithmetic and copies ran while one was open for 12% -> 1% of each run, Pallas kernels for 0% -> 11%
where the time goes in v1:
time: 202 us; the launch traced here: 201 us
  blocking collectives  79.5 us (39%)
  waiting for transfers between devices  49.6 us (25%)
  Pallas kernels  32.8 us (16%)
  starting transfers between devices  29.9 us (15%)
  other arithmetic  4.57 us (2%)
  local copies, waits for them, and re-layouts  4.27 us (2%)
    all_to_all x2, blocking collectives, swap(): return lax.all_to_all(x, axis, split_axis=0, concat_axis=0, tiled=True)  79.5 us
    all_to_all x4, waiting for transfers between devices, swap(): return lax.all_to_all(x, axis, split_axis=0, concat_axis=0, tiled=True)  49.6 us
    all_to_all x4, starting transfers between devices, swap(): return lax.all_to_all(x, axis, split_axis=0, concat_axis=0, tiled=True)  29.9 us
    pallas_call x2, Pallas kernels, attention_grads(): pl.pallas_call(kernel, grid=(steps,), in_specs=[pl.BlockSpec((per, 2 * pa...  28 us
    unnamed x8, local copies, waits for them, and re-layouts  4.27 us
  transfers between devices with their start and end apart: 4, of which 3 were waited for; matrix products, arithmetic and copies ran while one was open for 1% of the time, Pallas kernels for 11%

profile of v1, /device:TPU:1, one launch (start us, length us, event | category | flops | bytes accessed | tf_op | source)
XLA Modules:
  0.0 201.5 jit_solution(8602373880541081131)
XLA Ops:
  0.6 3.9 %by_head.1 = (bf16[32,200,128]{2,1,0:T(8,128)(2,1)}, bf16[32,64,128]{2,1,0:T(8,128)(2,1)}) custom-call(bf16[128,4096]{1,0:T(8,128)(2,1)} %bitcast.25, bf16[128,4096]{1,0:T(8,128)(2,1)} %bitcast.26, bf16[2,4096]{1,0:T(2,128)(2,1)} %bitcast.29, bf16[2,4096]{1,0:T(2,128)(2,1)} %bitcast.30), custom_call_target="tpu_custom_call" | custom-call | bytes 4194304 | tf_op jit(solution)/shard_map/by_head/pallas_call | solution.py:53
  4.5 51.2 %all_to_all.30.x_ref.refs_0_ = bf16[32,200,128]{2,1,0:T(8,128)(2,1)S(1)} all-to-all(bf16[32,200,128]{2,1,0:T(8,128)(2,1)} %get-tuple-element.13), channel_id=1, replica_groups=mesh['doc'=16,'ctx'=32] {'ctx'}, dimensions={0} | all-to-all | bytes 3276800 | tf_op jit(solution)/shard_map/all_to_all | solution.py:236
  55.7 0.1 memory_copies.1
  55.8 28.3 %all_to_all.31.refs_1_ = bf16[16,128,128]{2,1,0:T(8,128)(2,1)} all-to-all(bf16[16,128,128]{2,1,0:T(8,128)(2,1)S(1)} %memory_copies.1), channel_id=1, replica_groups=mesh['doc'=16,'ctx'=32] {'doc'}, dimensions={0} | all-to-all | bytes 1048576 | tf_op jit(solution)/shard_map/all_to_all | solution.py:236
  84.2 6.6 %all-to-all-start.3 = ((bf16[32,64,128]{2,1,0:T(8,128)(2,1)}), bf16[32,64,128]{2,1,0:T(8,128)(2,1)}, u32[]{:S(2)}, u32[]{:S(2)}) async-start(bf16[32,64,128]{2,1,0:T(8,128)(2,1)} %get-tuple-element.15), calls=%async_computation.3 | async-start | bytes 1048576 | tf_op jit(solution)/shard_map/all_to_all | solution.py:236
  90.7 0.0 copy-start
  90.8 1.0 copy-done
  91.8 20.9 %attention_grads.2 = (f32[3072,128]{1,0:T(8,128)S(1)}, f32[1,128]{1,0:T(1,128)S(1)}, f32[16,128,128]{2,1,0:T(8,128)S(1)}) custom-call(bf16[32,200,128]{2,1,0:T(8,128)(2,1)S(1)} %all_to_all.30.x_ref.refs_0_, bf16[16,128,128]{2,1,0:T(8,128)(2,1)S(1)} %copy-done), custom_call_target="tpu_custom_call" | custom-call | flops 6442450944 | bytes 3145728 | tf_op jit(solution)/shard_map/attention_grads/pallas_call | solution.py:160
  112.7 0.0 copy-start.2
  112.7 1.0 copy-done.2
  113.6 0.0 all-to-all-done.3.refs_0_
  113.6 0.0 copy-start.1
  113.6 1.0 copy-done.1
  114.7 0.0 copy-start.3
  114.7 1.2 copy-done.3
  115.9 7.1 %attention_grads.3 = (f32[1024,128]{1,0:T(8,128)S(1)}, f32[1,128]{1,0:T(1,128)S(1)}, f32[16,136,128]{2,1,0:T(8,128)S(1)}) custom-call(bf16[32,64,128]{2,1,0:T(8,128)(2,1)} %all-to-all-done.3.refs_0_, bf16[16,128,128]{2,1,0:T(8,128)(2,1)S(1)} %copy-done.1, f32[16,128,128]{2,1,0:T(8,128)S(1)} %copy-done.3), custom_call_target="tpu_custom_call" | custom-call | flops 2147483648 | bytes 1048576 | tf_op jit(solution)/shard_map/attention_grads/pallas_call | solution.py:160
  123.0 0.9 convert_element_type.25
  123.9 5.6 %all-to-all-start.4 = ((f16[16,136,128]{2,1,0:T(8,128)(2,1)}), f16[16,136,128]{2,1,0:T(8,128)(2,1)S(1)}, u32[]{:S(2)}, u32[]{:S(2)}) async-start(f16[16,136,128]{2,1,0:T(8,128)(2,1)} %convert_element_type.25), calls=%async_computation.4 | async-start | bytes 1114112 | tf_op jit(solution)/shard_map/all_to_all | solution.py:236
  129.5 15.1 %all-to-all-done.4 = f16[16,136,128]{2,1,0:T(8,128)(2,1)S(1)} async-done(((f16[16,136,128]{2,1,0:T(8,128)(2,1)}), f16[16,136,128]{2,1,0:T(8,128)(2,1)S(1)}, u32[]{:S(2)}, u32[]{:S(2)}) %all-to-all-start.4) | async-done | bytes 557088 | tf_op jit(solution)/shard_map/all_to_all | solution.py:236
  144.6 0.1 convert_element_type.26.x_ref
  144.6 0.2 memory_sums.1
  144.9 0.9 pad_maximum_fusion
  145.7 14.1 %all-to-all-start.5 = ((f16[32,48,128]{2,1,0:T(8,128)(2,1)}), f16[32,48,128]{2,1,0:T(8,128)(2,1)S(1)}, u32[]{:S(2)}, u32[]{:S(2)}) async-start(f16[32,48,128]{2,1,0:T(8,128)(2,1)} %pad_maximum_fusion), calls=%async_computation.5 | async-start | bytes 786432 | tf_op jit(solution)/shard_map/all_to_all | solution.py:236
  159.8 1.0 convert_element_type.22
  160.8 13.0 %all-to-all-done.5 = f16[32,48,128]{2,1,0:T(8,128)(2,1)S(1)} async-done(((f16[32,48,128]{2,1,0:T(8,128)(2,1)}), f16[32,48,128]{2,1,0:T(8,128)(2,1)S(1)}, u32[]{:S(2)}, u32[]{:S(2)}) %all-to-all-start.5) | async-done | bytes 393248 | tf_op jit(solution)/shard_map/all_to_all | solution.py:236
  173.8 3.7 %all-to-all-start.2 = ((f16[32,96,128]{2,1,0:T(8,128)(2,1)}), f16[32,96,128]{2,1,0:T(8,128)(2,1)S(1)}, u32[]{:S(2)}, u32[]{:S(2)}) async-start(f16[32,96,128]{2,1,0:T(8,128)(2,1)} %bitcast.4), calls=%async_computation.2 | async-start | bytes 1572864 | tf_op jit(solution)/shard_map/all_to_all | solution.py:236
  177.6 0.7 memory_rows.1
  178.4 21.5 %all-to-all-done.2 = f16[32,96,128]{2,1,0:T(8,128)(2,1)S(1)} async-done(((f16[32,96,128]{2,1,0:T(8,128)(2,1)}), f16[32,96,128]{2,1,0:T(8,128)(2,1)S(1)}, u32[]{:S(2)}, u32[]{:S(2)}) %all-to-all-start.2) | async-done | bytes 786464 | tf_op jit(solution)/shard_map/all_to_all | solution.py:236
  199.9 0.1 copy_bitcast_fusion
  200.0 1.5 maximum_bitcast_fusion
  (5 shorter events, 0.2 us)
Async XLA Ops:
  84.2 29.5 %all-to-all-start.3 = ((bf16[32,64,128]{2,1,0:T(8,128)(2,1)}), bf16[32,64,128]{2,1,0:T(8,128)(2,1)}, u32[]{:S(2)}, u32[]{:S(2)}) async-start(bf16[32,64,128]{2,1,0:T(8,128)(2,1)} %get-tuple-element.15), calls=%async_computation.3 | async-start | bytes 1048576 | tf_op jit(solution)/shard_map/all_to_all | solution.py:236
  90.7 1.0 copy-start
  112.7 1.0 copy-start.2
  113.6 1.0 copy-start.1
  114.7 1.2 copy-start.3
  123.9 20.7 %all-to-all-start.4 = ((f16[16,136,128]{2,1,0:T(8,128)(2,1)}), f16[16,136,128]{2,1,0:T(8,128)(2,1)S(1)}, u32[]{:S(2)}, u32[]{:S(2)}) async-start(f16[16,136,128]{2,1,0:T(8,128)(2,1)} %convert_element_type.25), calls=%async_computation.4 | async-start | bytes 1114112 | tf_op jit(solution)/shard_map/all_to_all | solution.py:236
  145.7 28.1 %all-to-all-start.5 = ((f16[32,48,128]{2,1,0:T(8,128)(2,1)}), f16[32,48,128]{2,1,0:T(8,128)(2,1)S(1)}, u32[]{:S(2)}, u32[]{:S(2)}) async-start(f16[32,48,128]{2,1,0:T(8,128)(2,1)} %pad_maximum_fusion), calls=%async_computation.5 | async-start | bytes 786432 | tf_op jit(solution)/shard_map/all_to_all | solution.py:236
  173.8 26.0 %all-to-all-start.2 = ((f16[32,96,128]{2,1,0:T(8,128)(2,1)}), f16[32,96,128]{2,1,0:T(8,128)(2,1)S(1)}, u32[]{:S(2)}, u32[]{:S(2)}) async-start(f16[32,96,128]{2,1,0:T(8,128)(2,1)} %bitcast.4), calls=%async_computation.2 | async-start | bytes 1572864 | tf_op jit(solution)/shard_map/all_to_all | solution.py:236

commit v2 on v1

--- a/solution.py
+++ b/solution.py
@@ -8,7 +8,7 @@
 
 HD = 128
 SCALE = HD ** (-0.5)
-CHUNKS = (96, 32)
+CHUNKS = (32, 96)
 QBLOCK = 512
 TILE = 8
 HALF_BITS = 14.0
@@ -30,16 +30,15 @@
     return jnp.ceil(jnp.log2(jnp.maximum(top, 1e-30))) - HALF_BITS
 
 
-def by_head(queries, out_grad, mem_keys, mem_values, chunks):
+def by_head(queries, out_grad, memory, chunks):
     rows, width = queries.shape
-    mem = mem_keys.shape[0]
+    mem = memory[0].shape[0]
     nheads = width // HD
     group = min(nheads, 8)
 
-    def kernel(q_ref, g_ref, k_ref, v_ref, *outs):
-        k = k_ref[...].astype(F32)
-        v = v_ref[...].astype(F32)
-        fill = jnp.zeros((TILE - 2 * mem, HD), F32)
+    def kernel(q_ref, g_ref, *refs):
+        held = [ref[...].astype(F32) for ref in refs[:4]]
+        outs = refs[4:]
         for h in range(group):
             cols = slice(h * HD, (h + 1) * HD)
             start = 0
@@ -47,50 +46,67 @@
                 out[h, :part, :] = q_ref[start:start + part, cols]
                 out[h, part:2 * part, :] = g_ref[start:start + part, cols]
                 start += part
-            outs[0][h, 2 * chunks[0]:, :] = jnp.concatenate([k[:, cols], v[:, cols], fill], axis=0).astype(BF16)
-
-    sizes = [2 * part + (TILE if c == 0 else 0) for c, part in enumerate(chunks)]
+            outs[0][h, 2 * chunks[0]:, :] = jnp.concatenate([x[:, cols] for x in held], axis=0).astype(BF16)
+
+    sizes = [2 * part + (4 * mem if c == 0 else 0) for c, part in enumerate(chunks)]
     return pl.pallas_call(
         kernel,
         grid=(nheads // group,),
         in_specs=[pl.BlockSpec((rows, group * HD), lambda i: (0, i))] * 2
-        + [pl.BlockSpec((mem, group * HD), lambda i: (0, i))] * 2,
+        + [pl.BlockSpec((mem, group * HD), lambda i: (0, i))] * 4,
         out_specs=[pl.BlockSpec((group, size, HD), lambda i: (i, 0, 0)) for size in sizes],
         out_shape=[jax.ShapeDtypeStruct((nheads, size, HD), BF16) for size in sizes],
         cost_estimate=pl.CostEstimate(flops=0, bytes_accessed=8 * rows * width, transcendentals=0),
         name="by_head",
-    )(queries, out_grad, mem_keys, mem_values)
-
-
-def memory_copies(block, part, rows, ndoc):
+    )(queries, out_grad, *memory)
+
+
+def held_memory(block, part, rows):
     ndev = block.shape[0]
     total = ndev * rows
 
     def kernel(x_ref, out, tmp):
         x = x_ref[...].astype(F32)
         for c in range(ndev):
-            tmp[c * rows:(c + 1) * rows, :] = x[c, :rows, :]
-            tmp[total + c * rows:total + (c + 1) * rows, :] = x[c, rows:2 * rows, :]
-        whole = tmp[...].astype(BF16)
-        for d in range(ndoc):
-            out[d] = whole
+            for t in range(4):
+                tmp[t * total + c * rows:t * total + (c + 1) * rows, :] = x[c, t * rows:(t + 1) * rows, :]
+        out[0] = tmp[:2 * total, :].astype(BF16)
+        out[1] = tmp[2 * total:, :].astype(BF16)
 
     return pl.pallas_call(
         kernel,
         grid=(1,),
-        in_specs=[pl.BlockSpec((ndev, TILE, HD), lambda i: (0, 2 * part // TILE, 0))],
-        out_specs=pl.BlockSpec((ndoc, 2 * total, HD), lambda i: (0, 0, 0)),
-        out_shape=jax.ShapeDtypeStruct((ndoc, 2 * total, HD), BF16),
-        scratch_shapes=[pltpu.VMEM((2 * total, HD), F32)],
-        cost_estimate=pl.CostEstimate(flops=0, bytes_accessed=4 * ndoc * total * HD, transcendentals=0),
+        in_specs=[pl.BlockSpec((ndev, 4 * rows, HD), lambda i: (0, 2 * part // (4 * rows), 0))],
+        out_specs=pl.BlockSpec((2, 2 * total, HD), lambda i: (0, 0, 0)),
+        out_shape=jax.ShapeDtypeStruct((2, 2 * total, HD), BF16),
+        scratch_shapes=[pltpu.VMEM((4 * total, HD), F32)],
+        cost_estimate=pl.CostEstimate(flops=0, bytes_accessed=16 * total * HD, transcendentals=0),
         compiler_params=pltpu.CompilerParams(vmem_limit_bytes=4 << 20),
-        name="memory_copies",
+        name="held_memory",
     )(block)
 
 
-def attention_grads(rows, part, memory, before, last):
+def flip(x, bit, ndoc):
+    return lax.ppermute(x, "doc", [(d, d ^ bit) for d in range(ndoc)])
+
+
+def gather_memory(held, ndoc):
+    places = [0, ndoc // 2]
+    bit = ndoc // 4
+    while True:
+        other = flip(held, bit, ndoc)
+        places = places + [p ^ bit for p in places]
+        if bit == 1:
+            return held, other, places
+        held = jnp.concatenate([held, other], axis=0)
+        bit //= 2
+
+
+def attention_grads(rows, part, doc, memory, before, last):
     ndev = rows.shape[0]
-    ndoc, both_mem, _ = memory.shape
+    held, other, places = memory
+    half, both_mem, _ = held.shape
+    ndoc = 2 * half
     mem = both_mem // 2
     total = ndoc * mem
     per = max(1, min(ndev, QBLOCK // part))
@@ -102,17 +118,20 @@
 
     def kernel(*refs):
         if before is None:
-            x_ref, m_ref, gq_ref, power_ref, sums_ref, k_ref, v_ref, top_ref = refs
+            d_ref, x_ref, m0_ref, m1_ref, gq_ref, power_ref, sums_ref, k_ref, v_ref, top_ref = refs
         else:
-            x_ref, m_ref, before_ref, gq_ref, power_ref, sums_ref, k_ref, v_ref, top_ref = refs
+            d_ref, x_ref, m0_ref, m1_ref, before_ref, gq_ref, power_ref, sums_ref, k_ref, v_ref, top_ref = refs
         acc_ref = sums_ref.at[:, :both_mem, :]
         step = pl.program_id(0)
 
         @pl.when(step == 0)
         def _():
             acc_ref[...] = jnp.zeros_like(acc_ref) if before is None else before_ref[...]
-            k_ref[...] = m_ref[:, :mem, :].reshape(total, HD)
-            v_ref[...] = m_ref[:, mem:, :].reshape(total, HD)
+            for r in range(ndoc):
+                m_ref = m0_ref if r < half else m1_ref
+                here = pl.ds(pl.multiple_of((d_ref[0] ^ places[r]) * mem, mem), mem)
+                k_ref[here, :] = m_ref[r % half, :mem, :]
+                v_ref[here, :] = m_ref[r % half, mem:, :]
             top_ref[...] = jnp.zeros_like(top_ref)
 
         q = x_ref[:, :part, :].reshape(block, HD)
@@ -156,12 +175,17 @@
     def whole(*shape):
         return pl.BlockSpec(shape, lambda i: (0,) * len(shape))
 
-    args = (rows, memory) if before is None else (rows, memory, before)
+    args = (doc, rows, held, other) if before is None else (doc, rows, held, other, before)
     return pl.pallas_call(
         kernel,
         grid=(steps,),
-        in_specs=[pl.BlockSpec((per, 2 * part, HD), lambda i: (i, 0, 0))]
-        + [whole(ndoc, both_mem, HD)] * (len(args) - 1),
+        in_specs=[
+            pl.BlockSpec(memory_space=pltpu.SMEM),
+            pl.BlockSpec((per, 2 * part, HD), lambda i: (i, 0, 0)),
+            whole(half, both_mem, HD),
+            whole(half, both_mem, HD),
+        ]
+        + [whole(ndoc, both_mem, HD)] * (len(args) - 4),
         out_specs=[whole(ndev * part, HD), whole(1, HD), whole(ndoc, size, HD)],
         out_shape=[
             jax.ShapeDtypeStruct((ndev * part, HD), F32),
@@ -241,15 +265,18 @@
     nctx = lax.axis_size("ctx")
     mem = mem_keys.shape[1]
     nchunks = len(CHUNKS)
-    blocks = list(by_head(queries[0], out_grad[0], mem_keys[0], mem_values[0], CHUNKS))
+    doc = lax.axis_index("doc").reshape(1)
+    memory = [mem_keys[0], mem_values[0]]
+    memory = memory + [flip(x, ndoc // 2, ndoc) for x in memory]
+    blocks = list(by_head(queries[0], out_grad[0], memory, CHUNKS))
     for i in range(nchunks):
         blocks[i] = swap(blocks[i], "ctx")
-    memory = swap(memory_copies(blocks[0], CHUNKS[0], mem, ndoc), "doc")
+    memory = gather_memory(held_memory(blocks[0], CHUNKS[0], mem), ndoc)
     sums = None
     powers = []
     grads = []
     for i, (block, part) in enumerate(zip(blocks, CHUNKS)):
-        grad_q, power, sums = attention_grads(block, part, memory, sums, i == nchunks - 1)
+        grad_q, power, sums = attention_grads(block, part, doc, memory, sums, i == nchunks - 1)
         powers.append(power)
         grads.append(grad_q.reshape(nctx, part, HD))
     sums = swap(sums.astype(HALF), "doc").astype(F32)

time: 202 us -> 197 us (0.975)
  blocking collectives: 79.5 us -> 25 us
  waiting for transfers between devices: 49.6 us -> 74.9 us
  starting transfers between devices: 29.9 us -> 54.6 us
    all_to_all x2 -> x1, blocking collectives: 79.5 us -> 25 us  [swap(): return lax.all_to_all(x, axis, split_axis=0, concat_axis=0, tiled=True)]
    ppermute x0 -> x5, starting transfers between devices: none -> 28.6 us  [flip(): return lax.ppermute(x, 'doc', [(d, d ^ bit) for d in range(ndoc)])]
    ppermute x0 -> x5, waiting for transfers between devices: none -> 22.4 us  [flip(): return lax.ppermute(x, 'doc', [(d, d ^ bit) for d in range(ndoc)])]
    all_to_all x4, starting transfers between devices: 29.9 us -> 26 us  [swap(): return lax.all_to_all(x, axis, split_axis=0, concat_axis=0, tiled=True)]
    all_to_all x4, waiting for transfers between devices: 49.6 us -> 52.5 us  [swap(): return lax.all_to_all(x, axis, split_axis=0, concat_axis=0, tiled=True)]
    unnamed x8 -> x12, local copies, waits for them, and re-layouts: 4.27 us -> 3.96 us
  transfers between devices with their start and end apart: 4 -> 9, of which waited for: 3 -> 7; matrix products, arithmetic and copies ran while one was open for 1% -> 1% of each run, Pallas kernels for 11% -> 3%
where the time goes in v2:
time: 197 us; the launch traced here: 196 us
  waiting for transfers between devices  74.9 us (38%)
  starting transfers between devices  54.6 us (28%)
  Pallas kernels  31.8 us (16%)
  blocking collectives  25 us (13%)
  other arithmetic  4.74 us (2%)
  local copies, waits for them, and re-layouts  3.96 us (2%)
    all_to_all x4, waiting for transfers between devices, swap(): return lax.all_to_all(x, axis, split_axis=0, concat_axis=0, tiled=True)  52.5 us
    ppermute x5, starting transfers between devices, flip(): return lax.ppermute(x, 'doc', [(d, d ^ bit) for d in range(ndoc)])  28.6 us
    pallas_call x2, Pallas kernels, attention_grads(): pl.pallas_call(kernel, grid=(steps,), in_specs=[pl.BlockSpec(memory_space...  26.9 us
    all_to_all x4, starting transfers between devices, swap(): return lax.all_to_all(x, axis, split_axis=0, concat_axis=0, tiled=True)  26 us
    all_to_all x1, blocking collectives, swap(): return lax.all_to_all(x, axis, split_axis=0, concat_axis=0, tiled=True)  25 us
    ppermute x5, waiting for transfers between devices, flip(): return lax.ppermute(x, 'doc', [(d, d ^ bit) for d in range(ndoc)])  22.4 us
    unnamed x12, local copies, waits for them, and re-layouts  3.96 us
  transfers between devices with their start and end apart: 9, of which 7 were waited for; matrix products, arithmetic and copies ran while one was open for 1% of the time, Pallas kernels for 3%

profile of v2, /device:TPU:1, one launch (start us, length us, event | category | flops | bytes accessed | tf_op | source)
XLA Modules:
  0.0 195.7 jit_solution(12498740663847534282)
XLA Ops:
  0.6 8.3 %collective-permute-start = (bf16[2,4096]{1,0:T(2,128)(2,1)}, bf16[2,4096]{1,0:T(2,128)(2,1)S(1)}, u32[]{:S(2)}, u32[]{:S(2)}) collective-permute-start(bf16[2,4096]{1,0:T(2,128)(2,1)} %bitcast.30), channel_id=1, source_target_pairs={{0,256},{32,288},{64,320},{96,352},{128,384},{160,416},{192,448},{... | collective-permute-start | bytes 49160 | tf_op jit(solution)/shard_map/ppermute | solution.py:90
  8.9 1.9 collective-permute-start.1
  10.8 0.0 collective-permute-done.refs_2_
  10.8 0.0 copy-start.4
  10.9 6.7 %collective-permute-done.1.refs_3_ = bf16[2,4096]{1,0:T(2,128)(2,1)S(1)} collective-permute-done((bf16[2,4096]{1,0:T(2,128)(2,1)}, bf16[2,4096]{1,0:T(2,128)(2,1)S(1)}, u32[]{:S(2)}, u32[]{:S(2)}) %collective-permute-start.1) | collective-permute-done | bytes 16416 | tf_op jit(solution)/shard_map/ppermute | solution.py:90
  17.6 0.0 copy-start.5
  17.6 0.0 copy-done.4
  17.6 0.6 copy-done.5
  18.2 3.9 %by_head.1 = (bf16[32,72,128]{2,1,0:T(8,128)(2,1)}, bf16[32,192,128]{2,1,0:T(8,128)(2,1)}) custom-call(bf16[128,4096]{1,0:T(8,128)(2,1)} %bitcast.26, bf16[128,4096]{1,0:T(8,128)(2,1)} %bitcast.27, bf16[2,4096]{1,0:T(2,128)(2,1)} %bitcast.31, bf16[2,4096]{1,0:T(2,128)(2,1)} %bitcast.33, bf16[2,4096]{1,0:T(2,128)(2,1)} %copy-done.4, bf16[2,4096]{1,0:T(2,128)(2,1)} %copy-done.5), custom_call_target="tpu_custom_call" | custom-call | bytes 4194304 | tf_op jit(solution)/shard_map/by_head/pallas_call | solution.py:52
  22.1 25.0 %all_to_all.25.x_ref.refs_1_ = bf16[32,72,128]{2,1,0:T(8,128)(2,1)S(1)} all-to-all(bf16[32,72,128]{2,1,0:T(8,128)(2,1)} %get-tuple-element.13), channel_id=1, replica_groups=mesh['doc'=16,'ctx'=32] {'ctx'}, dimensions={0} | all-to-all | bytes 1179648 | tf_op jit(solution)/shard_map/all_to_all | solution.py:260
  47.1 3.8 %all-to-all-start.2 = ((bf16[32,192,128]{2,1,0:T(8,128)(2,1)}), bf16[32,192,128]{2,1,0:T(8,128)(2,1)S(1)}, u32[]{:S(2)}, u32[]{:S(2)}) async-start(bf16[32,192,128]{2,1,0:T(8,128)(2,1)} %get-tuple-element.15), calls=%async_computation.2 | async-start | bytes 3145728 | tf_op jit(solution)/shard_map/all_to_all | solution.py:260
  50.8 0.1 held_memory.1
  50.9 10.6 %collective-permute-start.2 = (bf16[2,128,128]{2,1,0:T(8,128)(2,1)S(1)}, bf16[2,128,128]{2,1,0:T(8,128)(2,1)S(1)}, u32[]{:S(2)}, u32[]{:S(2)}) collective-permute-start(bf16[2,128,128]{2,1,0:T(8,128)(2,1)S(1)} %held_memory.1), channel_id=1, source_target_pairs={{0,128},{32,160},{64,192},{96,224},{128,0},{160,32},{192,64},{224,... | collective-permute-start | bytes 196616 | tf_op jit(solution)/shard_map/ppermute | solution.py:90
  61.6 2.2 %collective-permute-done.2 = bf16[2,128,128]{2,1,0:T(8,128)(2,1)S(1)} collective-permute-done((bf16[2,128,128]{2,1,0:T(8,128)(2,1)S(1)}, bf16[2,128,128]{2,1,0:T(8,128)(2,1)S(1)}, u32[]{:S(2)}, u32[]{:S(2)}) %collective-permute-start.2) | collective-permute-done | bytes 65568 | tf_op jit(solution)/shard_map/ppermute | solution.py:90
  63.7 5.8 %collective-permute-start.3 = (bf16[4,128,128]{2,1,0:T(8,128)(2,1)S(1)}, bf16[4,128,128]{2,1,0:T(8,128)(2,1)S(1)}, u32[]{:S(2)}, u32[]{:S(2)}) collective-permute-start(bf16[4,128,128]{2,1,0:T(8,128)(2,1)S(1)} %pad_maximum_fusion.2), channel_id=1, source_target_pairs={{0,64},{32,96},{64,0},{96,32},{128,192},{160,224},{192,128},{224,1... | collective-permute-start | bytes 393224 | tf_op jit(solution)/shard_map/ppermute | solution.py:90
  69.6 6.1 %collective-permute-done.3 = bf16[4,128,128]{2,1,0:T(8,128)(2,1)S(1)} collective-permute-done((bf16[4,128,128]{2,1,0:T(8,128)(2,1)S(1)}, bf16[4,128,128]{2,1,0:T(8,128)(2,1)S(1)}, u32[]{:S(2)}, u32[]{:S(2)}) %collective-permute-start.3) | collective-permute-done | bytes 131104 | tf_op jit(solution)/shard_map/ppermute | solution.py:90
  75.7 1.9 collective-permute-start.4
  77.7 7.4 %collective-permute-done.4.refs_3_ = bf16[8,128,128]{2,1,0:T(8,128)(2,1)S(1)} collective-permute-done((bf16[8,128,128]{2,1,0:T(8,128)(2,1)S(1)}, bf16[8,128,128]{2,1,0:T(8,128)(2,1)S(1)}, u32[]{:S(2)}, u32[]{:S(2)}) %collective-permute-start.4) | collective-permute-done | bytes 262176 | tf_op jit(solution)/shard_map/ppermute | solution.py:90
  85.0 6.1 %attention_grads.2 = (f32[1024,128]{1,0:T(8,128)S(1)}, f32[1,128]{1,0:T(1,128)S(1)}, f32[16,128,128]{2,1,0:T(8,128)S(1)}) custom-call(s32[1]{0:T(128)} %bitcast.refs_0_, bf16[32,72,128]{2,1,0:T(8,128)(2,1)S(1)} %all_to_all.25.x_ref.refs_1_, bf16[8,128,128]{2,1,0:T(8,128)(2,1)S(1)} %pad_maximum_fusion.1.refs_2_, ...), custom_call_target="tpu_custom_call" | custom-call | flops 2147483648 | bytes 1048576 | tf_op jit(solution)/shard_map/attention_grads/pallas_call | solution.py:179
  91.1 0.0 copy-start.2
  91.1 1.0 copy-done.2
  92.1 0.0 all-to-all-done.2.refs_1_
  92.1 0.0 copy-start.3
  92.1 1.2 copy-done.3
  93.3 20.9 %attention_grads.3 = (f32[3072,128]{1,0:T(8,128)S(1)}, f32[1,128]{1,0:T(1,128)S(1)}, f32[16,136,128]{2,1,0:T(8,128)S(1)}) custom-call(s32[1]{0:T(128)} %bitcast.refs_0_, bf16[32,192,128]{2,1,0:T(8,128)(2,1)S(1)} %all-to-all-done.2.refs_1_, bf16[8,128,128]{2,1,0:T(8,128)(2,1)S(1)} %pad_maximum_fusion.1.refs_2_, ...), custom_call_target="tpu_custom_call" | custom-call | flops 6442450944 | bytes 3145728 | tf_op jit(solution)/shard_map/attention_grads/pallas_call | solution.py:179
  114.2 0.0 copy-start
  114.2 1.1 copy-done
  115.3 0.0 copy-start.1
  115.3 0.9 convert_element_type.25
  116.2 10.1 %all-to-all-start.3 = ((f16[16,136,128]{2,1,0:T(8,128)(2,1)}), f16[16,136,128]{2,1,0:T(8,128)(2,1)S(1)}, u32[]{:S(2)}, u32[]{:S(2)}) async-start(f16[16,136,128]{2,1,0:T(8,128)(2,1)} %convert_element_type.25), calls=%async_computation.3 | async-start | bytes 1114112 | tf_op jit(solution)/shard_map/all_to_all | solution.py:260
  126.3 0.0 copy-done.1
  126.3 0.1 convert.7
  126.4 17.8 %all-to-all-done.3 = f16[16,136,128]{2,1,0:T(8,128)(2,1)S(1)} async-done(((f16[16,136,128]{2,1,0:T(8,128)(2,1)}), f16[16,136,128]{2,1,0:T(8,128)(2,1)S(1)}, u32[]{:S(2)}, u32[]{:S(2)}) %all-to-all-start.3) | async-done | bytes 557088 | tf_op jit(solution)/shard_map/all_to_all | solution.py:260
  144.2 0.1 convert_element_type.26.x_ref
  144.3 0.2 memory_sums.1
  144.5 1.2 pad_maximum_fusion
  145.7 8.4 %all-to-all-start.4 = ((f16[32,112,128]{2,1,0:T(8,128)(2,1)}), f16[32,112,128]{2,1,0:T(8,128)(2,1)S(1)}, u32[]{:S(2)}, u32[]{:S(2)}) async-start(f16[32,112,128]{2,1,0:T(8,128)(2,1)} %pad_maximum_fusion), calls=%async_computation.4 | async-start | bytes 1835008 | tf_op jit(solution)/shard_map/all_to_all | solution.py:260
  154.1 0.7 convert_element_type.22
  154.8 24.3 %all-to-all-done.4 = f16[32,112,128]{2,1,0:T(8,128)(2,1)S(1)} async-done(((f16[32,112,128]{2,1,0:T(8,128)(2,1)}), f16[32,112,128]{2,1,0:T(8,128)(2,1)S(1)}, u32[]{:S(2)}, u32[]{:S(2)}) %all-to-all-start.4) | async-done | bytes 917536 | tf_op jit(solution)/shard_map/all_to_all | solution.py:260
  179.1 3.8 %all-to-all-start.1 = ((f16[32,32,128]{2,1,0:T(8,128)(2,1)}), f16[32,32,128]{2,1,0:T(8,128)(2,1)S(1)}, u32[]{:S(2)}, u32[]{:S(2)}) async-start(f16[32,32,128]{2,1,0:T(8,128)(2,1)} %bitcast.5), calls=%async_computation.1 | async-start | bytes 524288 | tf_op jit(solution)/shard_map/all_to_all | solution.py:260
  183.0 0.7 memory_rows.1
  183.7 0.1 copy_bitcast_fusion
  183.9 10.4 %all-to-all-done.1 = f16[32,32,128]{2,1,0:T(8,128)(2,1)S(1)} async-done(((f16[32,32,128]{2,1,0:T(8,128)(2,1)}), f16[32,32,128]{2,1,0:T(8,128)(2,1)S(1)}, u32[]{:S(2)}, u32[]{:S(2)}) %all-to-all-start.1) | async-done | bytes 262176 | tf_op jit(solution)/shard_map/all_to_all | solution.py:260
  194.3 1.5 maximum_bitcast_fusion
  (6 shorter events, 0.2 us)
Async XLA Ops:
  0.6 10.2 %collective-permute-start = (bf16[2,4096]{1,0:T(2,128)(2,1)}, bf16[2,4096]{1,0:T(2,128)(2,1)S(1)}, u32[]{:S(2)}, u32[]{:S(2)}) collective-permute-start(bf16[2,4096]{1,0:T(2,128)(2,1)} %bitcast.30), channel_id=1, source_target_pairs={{0,256},{32,288},{64,320},{96,352},{128,384},{160,416},{192,448},{... | collective-permute-start | bytes 49160 | tf_op jit(solution)/shard_map/ppermute | solution.py:90
  8.9 8.7 %collective-permute-start.1 = (bf16[2,4096]{1,0:T(2,128)(2,1)}, bf16[2,4096]{1,0:T(2,128)(2,1)S(1)}, u32[]{:S(2)}, u32[]{:S(2)}) collective-permute-start(bf16[2,4096]{1,0:T(2,128)(2,1)} %bitcast.32), channel_id=1, source_target_pairs={{0,256},{32,288},{64,320},{96,352},{128,384},{160,416},{192,448},{... | collective-permute-start | bytes 49160 | tf_op jit(solution)/shard_map/ppermute | solution.py:90
  10.8 6.7 %copy-start.4 = (bf16[2,4096]{1,0:T(2,128)(2,1)}, bf16[2,4096]{1,0:T(2,128)(2,1)S(1)}, u32[]{:S(2)}) copy-start(bf16[2,4096]{1,0:T(2,128)(2,1)S(1)} %collective-permute-done.refs_2_) | copy-start | bytes 49156
  17.6 0.6 copy-start.5
  47.1 45.0 %all-to-all-start.2 = ((bf16[32,192,128]{2,1,0:T(8,128)(2,1)}), bf16[32,192,128]{2,1,0:T(8,128)(2,1)S(1)}, u32[]{:S(2)}, u32[]{:S(2)}) async-start(bf16[32,192,128]{2,1,0:T(8,128)(2,1)} %get-tuple-element.15), calls=%async_computation.2 | async-start | bytes 3145728 | tf_op jit(solution)/shard_map/all_to_all | solution.py:260
  50.9 12.8 %collective-permute-start.2 = (bf16[2,128,128]{2,1,0:T(8,128)(2,1)S(1)}, bf16[2,128,128]{2,1,0:T(8,128)(2,1)S(1)}, u32[]{:S(2)}, u32[]{:S(2)}) collective-permute-start(bf16[2,128,128]{2,1,0:T(8,128)(2,1)S(1)} %held_memory.1), channel_id=1, source_target_pairs={{0,128},{32,160},{64,192},{96,224},{128,0},{160,32},{192,64},{224,... | collective-permute-start | bytes 196616 | tf_op jit(solution)/shard_map/ppermute | solution.py:90
  63.7 12.0 %collective-permute-start.3 = (bf16[4,128,128]{2,1,0:T(8,128)(2,1)S(1)}, bf16[4,128,128]{2,1,0:T(8,128)(2,1)S(1)}, u32[]{:S(2)}, u32[]{:S(2)}) collective-permute-start(bf16[4,128,128]{2,1,0:T(8,128)(2,1)S(1)} %pad_maximum_fusion.2), channel_id=1, source_target_pairs={{0,64},{32,96},{64,0},{96,32},{128,192},{160,224},{192,128},{224,1... | collective-permute-start | bytes 393224 | tf_op jit(solution)/shard_map/ppermute | solution.py:90
  75.7 9.3 %collective-permute-start.4 = (bf16[8,128,128]{2,1,0:T(8,128)(2,1)S(1)}, bf16[8,128,128]{2,1,0:T(8,128)(2,1)S(1)}, u32[]{:S(2)}, u32[]{:S(2)}) collective-permute-start(bf16[8,128,128]{2,1,0:T(8,128)(2,1)S(1)} %pad_maximum_fusion.1.refs_2_), channel_id=1, source_target_pairs={{0,32},{32,0},{64,96},{96,64},{128,160},{160,128},{192,224},{224,1... | collective-permute-start | bytes 786440 | tf_op jit(solution)/shard_map/ppermute | solution.py:90
  91.1 1.0 copy-start.2
  92.1 1.2 copy-start.3
  114.2 1.1 copy-start
  115.3 11.0 %copy-start.1 = (f32[3072,128]{1,0:T(8,128)S(1)}, f32[3072,128]{1,0:T(8,128)}, u32[]{:S(2)}) copy-start(f32[3072,128]{1,0:T(8,128)} %copy-done) | copy-start | bytes 4718596
  116.2 28.0 %all-to-all-start.3 = ((f16[16,136,128]{2,1,0:T(8,128)(2,1)}), f16[16,136,128]{2,1,0:T(8,128)(2,1)S(1)}, u32[]{:S(2)}, u32[]{:S(2)}) async-start(f16[16,136,128]{2,1,0:T(8,128)(2,1)} %convert_element_type.25), calls=%async_computation.3 | async-start | bytes 1114112 | tf_op jit(solution)/shard_map/all_to_all | solution.py:260
  145.7 33.4 %all-to-all-start.4 = ((f16[32,112,128]{2,1,0:T(8,128)(2,1)}), f16[32,112,128]{2,1,0:T(8,128)(2,1)S(1)}, u32[]{:S(2)}, u32[]{:S(2)}) async-start(f16[32,112,128]{2,1,0:T(8,128)(2,1)} %pad_maximum_fusion), calls=%async_computation.4 | async-start | bytes 1835008 | tf_op jit(solution)/shard_map/all_to_all | solution.py:260
  179.1 15.1 %all-to-all-start.1 = ((f16[32,32,128]{2,1,0:T(8,128)(2,1)}), f16[32,32,128]{2,1,0:T(8,128)(2,1)S(1)}, u32[]{:S(2)}, u32[]{:S(2)}) async-start(f16[32,32,128]{2,1,0:T(8,128)(2,1)} %bitcast.5), calls=%async_computation.1 | async-start | bytes 524288 | tf_op jit(solution)/shard_map/all_to_all | solution.py:260

commit v3 on v2

--- a/solution.py
+++ b/solution.py
@@ -8,8 +8,8 @@
 
 HD = 128
 SCALE = HD ** (-0.5)
-CHUNKS = (32, 96)
-QBLOCK = 512
+CHUNKS = (48, 80)
+QBLOCK = 640
 TILE = 8
 HALF_BITS = 14.0
 F32 = jnp.float32
@@ -37,8 +37,9 @@
     group = min(nheads, 8)
 
     def kernel(q_ref, g_ref, *refs):
-        held = [ref[...].astype(F32) for ref in refs[:4]]
-        outs = refs[4:]
+        held = [ref[...].astype(F32) for ref in refs[:2]]
+        held.append(jnp.zeros((TILE - 2 * mem, held[0].shape[1]), F32))
+        outs = refs[2:]
         for h in range(group):
             cols = slice(h * HD, (h + 1) * HD)
             start = 0
@@ -48,12 +49,12 @@
                 start += part
             outs[0][h, 2 * chunks[0]:, :] = jnp.concatenate([x[:, cols] for x in held], axis=0).astype(BF16)
 
-    sizes = [2 * part + (4 * mem if c == 0 else 0) for c, part in enumerate(chunks)]
+    sizes = [2 * part + (TILE if c == 0 else 0) for c, part in enumerate(chunks)]
     return pl.pallas_call(
         kernel,
         grid=(nheads // group,),
         in_specs=[pl.BlockSpec((rows, group * HD), lambda i: (0, i))] * 2
-        + [pl.BlockSpec((mem, group * HD), lambda i: (0, i))] * 4,
+        + [pl.BlockSpec((mem, group * HD), lambda i: (0, i))] * 2,
         out_specs=[pl.BlockSpec((group, size, HD), lambda i: (i, 0, 0)) for size in sizes],
         out_shape=[jax.ShapeDtypeStruct((nheads, size, HD), BF16) for size in sizes],
         cost_estimate=pl.CostEstimate(flops=0, bytes_accessed=8 * rows * width, transcendentals=0),
@@ -61,40 +62,35 @@
     )(queries, out_grad, *memory)
 
 
-def held_memory(block, part, rows):
+def own_memory(block, part, rows):
     ndev = block.shape[0]
     total = ndev * rows
 
     def kernel(x_ref, out, tmp):
         x = x_ref[...].astype(F32)
         for c in range(ndev):
-            for t in range(4):
-                tmp[t * total + c * rows:t * total + (c + 1) * rows, :] = x[c, t * rows:(t + 1) * rows, :]
-        out[0] = tmp[:2 * total, :].astype(BF16)
-        out[1] = tmp[2 * total:, :].astype(BF16)
+            tmp[c * rows:(c + 1) * rows, :] = x[c, :rows, :]
+            tmp[total + c * rows:total + (c + 1) * rows, :] = x[c, rows:2 * rows, :]
+        out[0] = tmp[...].astype(BF16)
 
     return pl.pallas_call(
         kernel,
         grid=(1,),
-        in_specs=[pl.BlockSpec((ndev, 4 * rows, HD), lambda i: (0, 2 * part // (4 * rows), 0))],
-        out_specs=pl.BlockSpec((2, 2 * total, HD), lambda i: (0, 0, 0)),
-        out_shape=jax.ShapeDtypeStruct((2, 2 * total, HD), BF16),
-        scratch_shapes=[pltpu.VMEM((4 * total, HD), F32)],
-        cost_estimate=pl.CostEstimate(flops=0, bytes_accessed=16 * total * HD, transcendentals=0),
+        in_specs=[pl.BlockSpec((ndev, TILE, HD), lambda i: (0, 2 * part // TILE, 0))],
+        out_specs=pl.BlockSpec((1, 2 * total, HD), lambda i: (0, 0, 0)),
+        out_shape=jax.ShapeDtypeStruct((1, 2 * total, HD), BF16),
+        scratch_shapes=[pltpu.VMEM((2 * total, HD), F32)],
+        cost_estimate=pl.CostEstimate(flops=0, bytes_accessed=8 * total * HD, transcendentals=0),
         compiler_params=pltpu.CompilerParams(vmem_limit_bytes=4 << 20),
-        name="held_memory",
+        name="own_memory",
     )(block)
 
 
-def flip(x, bit, ndoc):
-    return lax.ppermute(x, "doc", [(d, d ^ bit) for d in range(ndoc)])
-
-
 def gather_memory(held, ndoc):
-    places = [0, ndoc // 2]
-    bit = ndoc // 4
+    places = [0]
+    bit = ndoc // 2
     while True:
-        other = flip(held, bit, ndoc)
+        other = lax.ppermute(held, "doc", [(d, d ^ bit) for d in range(ndoc)])
         places = places + [p ^ bit for p in places]
         if bit == 1:
             return held, other, places
@@ -118,9 +114,9 @@
 
     def kernel(*refs):
         if before is None:
-            d_ref, x_ref, m0_ref, m1_ref, gq_ref, power_ref, sums_ref, k_ref, v_ref, top_ref = refs
+            d_ref, x_ref, m0_ref, m1_ref, gq_ref, power_ref, sums_ref, k_ref, v_ref, kt_ref, top_ref = refs
         else:
-            d_ref, x_ref, m0_ref, m1_ref, before_ref, gq_ref, power_ref, sums_ref, k_ref, v_ref, top_ref = refs
+            d_ref, x_ref, m0_ref, m1_ref, before_ref, gq_ref, power_ref, sums_ref, k_ref, v_ref, kt_ref, top_ref = refs
         acc_ref = sums_ref.at[:, :both_mem, :]
         step = pl.program_id(0)
 
@@ -132,6 +128,7 @@
                 here = pl.ds(pl.multiple_of((d_ref[0] ^ places[r]) * mem, mem), mem)
                 k_ref[here, :] = m_ref[r % half, :mem, :]
                 v_ref[here, :] = m_ref[r % half, mem:, :]
+            kt_ref[...] = jnp.transpose(k_ref[...].astype(F32)).astype(BF16)
             top_ref[...] = jnp.zeros_like(top_ref)
 
         q = x_ref[:, :part, :].reshape(block, HD)
@@ -148,7 +145,8 @@
         s_hi, s_lo = split(dscore)
         grad_v = dot(p_hi, g, 1, 0) + dot(p_lo, g, 1, 0)
         grad_k = (dot(s_hi, q, 1, 0) + dot(s_lo, q, 1, 0)) * SCALE
-        grad_q = (dot(s_hi, k, 0, 0) + dot(s_lo, k, 0, 0)) * SCALE
+        kt = kt_ref[...]
+        grad_q = jnp.transpose(dot(kt, s_hi, 1, 0) + dot(kt, s_lo, 1, 0)) * SCALE
         gq_ref[pl.ds(pl.multiple_of(step * block, block), block), :] = grad_q
         top_ref[...] = jnp.maximum(top_ref[...], jnp.max(jnp.abs(grad_q), axis=0, keepdims=True))
         acc_ref[:, :mem, :] += grad_k.reshape(ndoc, mem, HD)
@@ -192,7 +190,12 @@
             jax.ShapeDtypeStruct((1, HD), F32),
             jax.ShapeDtypeStruct((ndoc, size, HD), F32),
         ],
-        scratch_shapes=[pltpu.VMEM((total, HD), BF16)] * 2 + [pltpu.VMEM((1, HD), F32)],
+        scratch_shapes=[
+            pltpu.VMEM((total, HD), BF16),
+            pltpu.VMEM((total, HD), BF16),
+            pltpu.VMEM((HD, total), BF16),
+            pltpu.VMEM((1, HD), F32),
+        ],
         cost_estimate=pl.CostEstimate(
             flops=16 * ndev * part * total * HD,
             bytes_accessed=8 * ndev * part * HD,
@@ -266,12 +269,10 @@
     mem = mem_keys.shape[1]
     nchunks = len(CHUNKS)
     doc = lax.axis_index("doc").reshape(1)
-    memory = [mem_keys[0], mem_values[0]]
-    memory = memory + [flip(x, ndoc // 2, ndoc) for x in memory]
-    blocks = list(by_head(queries[0], out_grad[0], memory, CHUNKS))
+    blocks = list(by_head(queries[0], out_grad[0], [mem_keys[0], mem_values[0]], CHUNKS))
     for i in range(nchunks):
         blocks[i] = swap(blocks[i], "ctx")
-    memory = gather_memory(held_memory(blocks[0], CHUNKS[0], mem), ndoc)
+    memory = gather_memory(own_memory(blocks[0], CHUNKS[0], mem), ndoc)
     sums = None
     powers = []
     grads = []

time: 197 us -> 206 us (1.046)
  blocking collectives: 25 us -> 34.2 us
  waiting for transfers between devices: 74.9 us -> 83.8 us
  starting transfers between devices: 54.6 us -> 47.3 us
  Pallas kernels: 31.8 us -> 29.2 us
    ppermute x5 -> x4, waiting for transfers between devices: 22.4 us -> 35.8 us  [gather_memory(): other = lax.ppermute(held, 'doc', [(d, d ^ bit) for d in range(ndoc)])]
    all_to_all x1, blocking collectives: 25 us -> 34.2 us  [swap(): return lax.all_to_all(x, axis, split_axis=0, concat_axis=0, tiled=True)]
    ppermute x5 -> x4, starting transfers between devices: 28.6 us -> 21.3 us  [gather_memory(): other = lax.ppermute(held, 'doc', [(d, d ^ bit) for d in range(ndoc)])]
    all_to_all x4, waiting for transfers between devices: 52.5 us -> 47.9 us  [swap(): return lax.all_to_all(x, axis, split_axis=0, concat_axis=0, tiled=True)]
    pallas_call x2, Pallas kernels: 26.9 us -> 24.4 us  [attention_grads(): pl.pallas_call(kernel, grid=(steps,), in_specs=[pl.BlockSpec(memory_space...]
    unnamed x12 -> x16, local copies, waits for them, and re-layouts: 3.96 us -> 5.02 us
  transfers between devices with their start and end apart: 9 -> 8, of which waited for: 7 -> 7; matrix products, arithmetic and copies ran while one was open for 1% -> 1% of each run, Pallas kernels for 3% -> 5%
where the time goes in v3:
time: 206 us; the launch traced here: 205 us
  waiting for transfers between devices  83.8 us (41%)
  starting transfers between devices  47.3 us (23%)
  blocking collectives  34.2 us (17%)
  Pallas kernels  29.2 us (14%)
  local copies, waits for them, and re-layouts  5.02 us (2%)
  other arithmetic  4.7 us (2%)
    all_to_all x4, waiting for transfers between devices, swap(): return lax.all_to_all(x, axis, split_axis=0, concat_axis=0, tiled=True)  47.9 us
    ppermute x4, waiting for transfers between devices, gather_memory(): other = lax.ppermute(held, 'doc', [(d, d ^ bit) for d in range(ndoc)])  35.8 us
    all_to_all x1, blocking collectives, swap(): return lax.all_to_all(x, axis, split_axis=0, concat_axis=0, tiled=True)  34.2 us
    all_to_all x4, starting transfers between devices, swap(): return lax.all_to_all(x, axis, split_axis=0, concat_axis=0, tiled=True)  26 us
    pallas_call x2, Pallas kernels, attention_grads(): pl.pallas_call(kernel, grid=(steps,), in_specs=[pl.BlockSpec(memory_space...  24.4 us
    ppermute x4, starting transfers between devices, gather_memory(): other = lax.ppermute(held, 'doc', [(d, d ^ bit) for d in range(ndoc)])  21.3 us
    unnamed x16, local copies, waits for them, and re-layouts  5.02 us
  transfers between devices with their start and end apart: 8, of which 7 were waited for; matrix products, arithmetic and copies ran while one was open for 1% of the time, Pallas kernels for 5%

profile of v3, /device:TPU:1, one launch (start us, length us, event | category | flops | bytes accessed | tf_op | source)
XLA Modules:
  0.0 205.0 jit_solution(1418005295339030525)
XLA Ops:
  0.6 3.9 %by_head.1 = (bf16[32,104,128]{2,1,0:T(8,128)(2,1)}, bf16[32,160,128]{2,1,0:T(8,128)(2,1)}) custom-call(bf16[128,4096]{1,0:T(8,128)(2,1)} %bitcast.26, bf16[128,4096]{1,0:T(8,128)(2,1)} %bitcast.27, bf16[2,4096]{1,0:T(2,128)(2,1)} %bitcast.30, bf16[2,4096]{1,0:T(2,128)(2,1)} %bitcast.31), custom_call_target="tpu_custom_call" | custom-call | bytes 4194304 | tf_op jit(solution)/shard_map/by_head/pallas_call | solution.py:53
  4.5 34.2 %all_to_all.25.x_ref.refs_1_ = bf16[32,104,128]{2,1,0:T(8,128)(2,1)S(1)} all-to-all(bf16[32,104,128]{2,1,0:T(8,128)(2,1)} %get-tuple-element.13), channel_id=1, replica_groups=mesh['doc'=16,'ctx'=32] {'ctx'}, dimensions={0} | all-to-all | bytes 1703936 | tf_op jit(solution)/shard_map/all_to_all | solution.py:263
  38.7 3.8 %all-to-all-start.2 = ((bf16[32,160,128]{2,1,0:T(8,128)(2,1)}), bf16[32,160,128]{2,1,0:T(8,128)(2,1)S(1)}, u32[]{:S(2)}, u32[]{:S(2)}) async-start(bf16[32,160,128]{2,1,0:T(8,128)(2,1)} %get-tuple-element.15), calls=%async_computation.2 | async-start | bytes 2621440 | tf_op jit(solution)/shard_map/all_to_all | solution.py:263
  42.6 3.2 %collective-permute-start = (bf16[1,128,128]{2,1,0:T(8,128)(2,1)S(1)}, bf16[1,128,128]{2,1,0:T(8,128)(2,1)S(1)}, u32[]{:S(2)}, u32[]{:S(2)}) collective-permute-start(bf16[1,128,128]{2,1,0:T(8,128)(2,1)S(1)} %own_memory.1), channel_id=1, source_target_pairs={{0,256},{32,288},{64,320},{96,352},{128,384},{160,416},{192,448},{... | collective-permute-start | bytes 98312 | tf_op jit(solution)/shard_map/ppermute | solution.py:93
  45.8 21.5 %collective-permute-done = bf16[1,128,128]{2,1,0:T(8,128)(2,1)S(1)} collective-permute-done((bf16[1,128,128]{2,1,0:T(8,128)(2,1)S(1)}, bf16[1,128,128]{2,1,0:T(8,128)(2,1)S(1)}, u32[]{:S(2)}, u32[]{:S(2)}) %collective-permute-start) | collective-permute-done | bytes 32800 | tf_op jit(solution)/shard_map/ppermute | solution.py:93
  67.3 10.3 %collective-permute-start.1 = (bf16[2,128,128]{2,1,0:T(8,128)(2,1)S(1)}, bf16[2,128,128]{2,1,0:T(8,128)(2,1)S(1)}, u32[]{:S(2)}, u32[]{:S(2)}) collective-permute-start(bf16[2,128,128]{2,1,0:T(8,128)(2,1)S(1)} %pad_maximum_fusion.3), channel_id=1, source_target_pairs={{0,128},{32,160},{64,192},{96,224},{128,0},{160,32},{192,64},{224,... | collective-permute-start | bytes 196616 | tf_op jit(solution)/shard_map/ppermute | solution.py:93
  77.7 1.7 collective-permute-done.1
  79.4 5.8 %collective-permute-start.2 = (bf16[4,128,128]{2,1,0:T(8,128)(2,1)S(1)}, bf16[4,128,128]{2,1,0:T(8,128)(2,1)S(1)}, u32[]{:S(2)}, u32[]{:S(2)}) collective-permute-start(bf16[4,128,128]{2,1,0:T(8,128)(2,1)S(1)} %pad_maximum_fusion.2), channel_id=1, source_target_pairs={{0,64},{32,96},{64,0},{96,32},{128,192},{160,224},{192,128},{224,1... | collective-permute-start | bytes 393224 | tf_op jit(solution)/shard_map/ppermute | solution.py:93
  85.2 5.7 %collective-permute-done.2 = bf16[4,128,128]{2,1,0:T(8,128)(2,1)S(1)} collective-permute-done((bf16[4,128,128]{2,1,0:T(8,128)(2,1)S(1)}, bf16[4,128,128]{2,1,0:T(8,128)(2,1)S(1)}, u32[]{:S(2)}, u32[]{:S(2)}) %collective-permute-start.2) | collective-permute-done | bytes 131104 | tf_op jit(solution)/shard_map/ppermute | solution.py:93
  90.9 0.0 copy-start.2
  90.9 1.9 collective-permute-start.3
  92.8 6.9 %collective-permute-done.3.refs_3_ = bf16[8,128,128]{2,1,0:T(8,128)(2,1)S(1)} collective-permute-done((bf16[8,128,128]{2,1,0:T(8,128)(2,1)S(1)}, bf16[8,128,128]{2,1,0:T(8,128)(2,1)S(1)}, u32[]{:S(2)}, u32[]{:S(2)}) %collective-permute-start.3) | collective-permute-done | bytes 262176 | tf_op jit(solution)/shard_map/ppermute | solution.py:93
  99.8 0.0 copy-start.4
  99.8 9.9 %attention_grads.2 = (f32[1536,128]{1,0:T(8,128)S(1)}, f32[1,128]{1,0:T(1,128)S(1)}, f32[16,128,128]{2,1,0:T(8,128)S(1)}) custom-call(s32[1]{0:T(128)} %bitcast.refs_0_, bf16[32,104,128]{2,1,0:T(8,128)(2,1)S(1)} %all_to_all.25.x_ref.refs_1_, bf16[8,128,128]{2,1,0:T(8,128)(2,1)S(1)} %pad_maximum_fusion.1.refs_2_, ...), custom_call_target="tpu_custom_call" | custom-call | flops 3221225472 | bytes 1572864 | tf_op jit(solution)/shard_map/attention_grads/pallas_call | solution.py:177
  109.6 0.0 copy-done.2
  109.6 0.0 copy-done.4
  109.7 0.0 copy-start
  109.7 0.9 copy-done
  110.6 0.0 copy-start.6
  110.6 1.0 copy-done.6
  111.5 0.0 all-to-all-done.2.refs_1_
  111.5 0.0 copy-start.3
  111.5 0.9 copy-done.3
  112.5 0.0 copy-start.5
  112.5 0.9 copy-done.5
  113.4 0.0 copy-start.7
  113.4 1.2 copy-done.7
  114.7 14.5 %attention_grads.3 = (f32[2560,128]{1,0:T(8,128)S(1)}, f32[1,128]{1,0:T(1,128)S(1)}, f32[16,136,128]{2,1,0:T(8,128)S(1)}) custom-call(s32[1]{0:T(128)} %bitcast.refs_0_, bf16[32,160,128]{2,1,0:T(8,128)(2,1)S(1)} %all-to-all-done.2.refs_1_, bf16[8,128,128]{2,1,0:T(8,128)(2,1)S(1)} %copy-done.3, bf16[8,128,128]{2,1,0:T(8,128)(2,1)S(1)} %copy-done.5, ...), custom_call_target="tpu_custom_call" | custom-call | flops 5368709120 | bytes 2621440 | tf_op jit(solution)/shard_map/attention_grads/pallas_call | solution.py:177
  129.2 0.9 convert_element_type.25
  130.1 6.9 %all-to-all-start.3 = ((f16[16,136,128]{2,1,0:T(8,128)(2,1)}), f16[16,136,128]{2,1,0:T(8,128)(2,1)S(1)}, u32[]{:S(2)}, u32[]{:S(2)}) async-start(f16[16,136,128]{2,1,0:T(8,128)(2,1)} %convert_element_type.25), calls=%async_computation.3 | async-start | bytes 1114112 | tf_op jit(solution)/shard_map/all_to_all | solution.py:263
  137.0 0.1 convert.7
  137.1 13.3 %all-to-all-done.3 = f16[16,136,128]{2,1,0:T(8,128)(2,1)S(1)} async-done(((f16[16,136,128]{2,1,0:T(8,128)(2,1)}), f16[16,136,128]{2,1,0:T(8,128)(2,1)S(1)}, u32[]{:S(2)}, u32[]{:S(2)}) %all-to-all-start.3) | async-done | bytes 557088 | tf_op jit(solution)/shard_map/all_to_all | solution.py:263
  150.4 0.1 convert_element_type.26.x_ref
  150.4 0.2 memory_sums.1
  150.7 0.0 copy-start.1
  150.7 1.1 pad_maximum_fusion
  151.8 11.5 %all-to-all-start.4 = ((f16[32,96,128]{2,1,0:T(8,128)(2,1)}), f16[32,96,128]{2,1,0:T(8,128)(2,1)S(1)}, u32[]{:S(2)}, u32[]{:S(2)}) async-start(f16[32,96,128]{2,1,0:T(8,128)(2,1)} %pad_maximum_fusion), calls=%async_computation.4 | async-start | bytes 1572864 | tf_op jit(solution)/shard_map/all_to_all | solution.py:263
  163.3 0.0 copy-done.1
  163.3 0.8 convert_element_type.22
  164.1 21.5 %all-to-all-done.4 = f16[32,96,128]{2,1,0:T(8,128)(2,1)S(1)} async-done(((f16[32,96,128]{2,1,0:T(8,128)(2,1)}), f16[32,96,128]{2,1,0:T(8,128)(2,1)S(1)}, u32[]{:S(2)}, u32[]{:S(2)}) %all-to-all-start.4) | async-done | bytes 786464 | tf_op jit(solution)/shard_map/all_to_all | solution.py:263
  185.6 3.8 %all-to-all-start.1 = ((f16[32,48,128]{2,1,0:T(8,128)(2,1)}), f16[32,48,128]{2,1,0:T(8,128)(2,1)S(1)}, u32[]{:S(2)}, u32[]{:S(2)}) async-start(f16[32,48,128]{2,1,0:T(8,128)(2,1)} %bitcast.5), calls=%async_computation.1 | async-start | bytes 786432 | tf_op jit(solution)/shard_map/all_to_all | solution.py:263
  189.5 0.7 memory_rows.1
  190.2 0.1 copy_bitcast_fusion
  190.3 13.2 %all-to-all-done.1 = f16[32,48,128]{2,1,0:T(8,128)(2,1)S(1)} async-done(((f16[32,48,128]{2,1,0:T(8,128)(2,1)}), f16[32,48,128]{2,1,0:T(8,128)(2,1)S(1)}, u32[]{:S(2)}, u32[]{:S(2)}) %all-to-all-start.1) | async-done | bytes 393248 | tf_op jit(solution)/shard_map/all_to_all | solution.py:263
  203.4 0.1 copy_bitcast_fusion.1
  203.5 1.5 maximum_bitcast_fusion
  (7 shorter events, 0.2 us)
Async XLA Ops:
  38.7 72.8 %all-to-all-start.2 = ((bf16[32,160,128]{2,1,0:T(8,128)(2,1)}), bf16[32,160,128]{2,1,0:T(8,128)(2,1)S(1)}, u32[]{:S(2)}, u32[]{:S(2)}) async-start(bf16[32,160,128]{2,1,0:T(8,128)(2,1)} %get-tuple-element.15), calls=%async_computation.2 | async-start | bytes 2621440 | tf_op jit(solution)/shard_map/all_to_all | solution.py:263
  42.6 24.7 %collective-permute-start = (bf16[1,128,128]{2,1,0:T(8,128)(2,1)S(1)}, bf16[1,128,128]{2,1,0:T(8,128)(2,1)S(1)}, u32[]{:S(2)}, u32[]{:S(2)}) collective-permute-start(bf16[1,128,128]{2,1,0:T(8,128)(2,1)S(1)} %own_memory.1), channel_id=1, source_target_pairs={{0,256},{32,288},{64,320},{96,352},{128,384},{160,416},{192,448},{... | collective-permute-start | bytes 98312 | tf_op jit(solution)/shard_map/ppermute | solution.py:93
  67.3 12.1 %collective-permute-start.1 = (bf16[2,128,128]{2,1,0:T(8,128)(2,1)S(1)}, bf16[2,128,128]{2,1,0:T(8,128)(2,1)S(1)}, u32[]{:S(2)}, u32[]{:S(2)}) collective-permute-start(bf16[2,128,128]{2,1,0:T(8,128)(2,1)S(1)} %pad_maximum_fusion.3), channel_id=1, source_target_pairs={{0,128},{32,160},{64,192},{96,224},{128,0},{160,32},{192,64},{224,... | collective-permute-start | bytes 196616 | tf_op jit(solution)/shard_map/ppermute | solution.py:93
  79.4 11.5 %collective-permute-start.2 = (bf16[4,128,128]{2,1,0:T(8,128)(2,1)S(1)}, bf16[4,128,128]{2,1,0:T(8,128)(2,1)S(1)}, u32[]{:S(2)}, u32[]{:S(2)}) collective-permute-start(bf16[4,128,128]{2,1,0:T(8,128)(2,1)S(1)} %pad_maximum_fusion.2), channel_id=1, source_target_pairs={{0,64},{32,96},{64,0},{96,32},{128,192},{160,224},{192,128},{224,1... | collective-permute-start | bytes 393224 | tf_op jit(solution)/shard_map/ppermute | solution.py:93
  90.9 18.7 %copy-start.2 = (bf16[8,128,128]{2,1,0:T(8,128)(2,1)}, bf16[8,128,128]{2,1,0:T(8,128)(2,1)S(1)}, u32[]{:S(2)}) copy-start(bf16[8,128,128]{2,1,0:T(8,128)(2,1)S(1)} %pad_maximum_fusion.1.refs_2_) | copy-start | bytes 786436
  90.9 8.9 %collective-permute-start.3 = (bf16[8,128,128]{2,1,0:T(8,128)(2,1)S(1)}, bf16[8,128,128]{2,1,0:T(8,128)(2,1)S(1)}, u32[]{:S(2)}, u32[]{:S(2)}) collective-permute-start(bf16[8,128,128]{2,1,0:T(8,128)(2,1)S(1)} %pad_maximum_fusion.1.refs_2_), channel_id=1, source_target_pairs={{0,32},{32,0},{64,96},{96,64},{128,160},{160,128},{192,224},{224,1... | collective-permute-start | bytes 786440 | tf_op jit(solution)/shard_map/ppermute | solution.py:93
  99.8 9.9 %copy-start.4 = (bf16[8,128,128]{2,1,0:T(8,128)(2,1)}, bf16[8,128,128]{2,1,0:T(8,128)(2,1)S(1)}, u32[]{:S(2)}) copy-start(bf16[8,128,128]{2,1,0:T(8,128)(2,1)S(1)} %collective-permute-done.3.refs_3_) | copy-start | bytes 786436
  109.7 0.9 copy-start
  110.6 1.0 copy-start.6
  111.5 1.0 copy-start.3
  112.5 0.9 copy-start.5
  113.4 1.2 copy-start.7
  130.1 20.3 %all-to-all-start.3 = ((f16[16,136,128]{2,1,0:T(8,128)(2,1)}), f16[16,136,128]{2,1,0:T(8,128)(2,1)S(1)}, u32[]{:S(2)}, u32[]{:S(2)}) async-start(f16[16,136,128]{2,1,0:T(8,128)(2,1)} %convert_element_type.25), calls=%async_computation.3 | async-start | bytes 1114112 | tf_op jit(solution)/shard_map/all_to_all | solution.py:263
  150.7 12.6 %copy-start.1 = (f32[1536,128]{1,0:T(8,128)S(1)}, f32[1536,128]{1,0:T(8,128)}, u32[]{:S(2)}) copy-start(f32[1536,128]{1,0:T(8,128)} %copy-done) | copy-start | bytes 2359300
  151.8 33.9 %all-to-all-start.4 = ((f16[32,96,128]{2,1,0:T(8,128)(2,1)}), f16[32,96,128]{2,1,0:T(8,128)(2,1)S(1)}, u32[]{:S(2)}, u32[]{:S(2)}) async-start(f16[32,96,128]{2,1,0:T(8,128)(2,1)} %pad_maximum_fusion), calls=%async_computation.4 | async-start | bytes 1572864 | tf_op jit(solution)/shard_map/all_to_all | solution.py:263
  185.6 17.8 %all-to-all-start.1 = ((f16[32,48,128]{2,1,0:T(8,128)(2,1)}), f16[32,48,128]{2,1,0:T(8,128)(2,1)S(1)}, u32[]{:S(2)}, u32[]{:S(2)}) async-start(f16[32,48,128]{2,1,0:T(8,128)(2,1)} %bitcast.5), calls=%async_computation.1 | async-start | bytes 786432 | tf_op jit(solution)/shard_map/all_to_all | solution.py:263
